TPU v7x, 32 devices: a whole 2x2x4 slice. The times are simulated.
32 devices in a mesh: row: 4 (over y, x), col: 8 (over z, core).
Axes of the slice: x: 2, y: 2, z: 4, core: 2. Of those that a mesh axis runs over, the one named last changes fastest.
Arguments:
- tokens: bfloat16 [32, 512, 960], P(('row', 'col')), may hold values from -6 to 6
- segment_ids: int32 [32, 512], P(('row', 'col')), may hold values from 0 to 3, never falling along the last dimension, each value on 1 to 320 neighbouring positions
- route_one: int32 [32, 384], P(('row', 'col')), may hold values from 0 to 511, as said below
- route_two: int32 [32, 256], P(('row', 'col')), may hold values from 0 to 511, as said below
- route_three: int32 [32, 128], P(('row', 'col')), may hold values from 0 to 511, as said below
- attn_gain: bfloat16 [960], P('row'), may hold values from 0.5 to 1.5
- router: bfloat16 [960, 3], P('row'), may hold values from -0.125 to 0.125
- w_query: bfloat16 [960, 960], P('row', 'col'), may hold values from -0.1875 to 0.1875
- w_key: bfloat16 [960, 320], P('row', 'col'), may hold values from -0.1875 to 0.1875
- w_value: bfloat16 [960, 320], P('row', 'col'), may hold values from -0.1875 to 0.1875
- w_out: bfloat16 [960, 960], P('row', 'col'), may hold values from -0.75 to 0.75
- ffn_gain: bfloat16 [960], P('row'), may hold values from 0.5 to 1.5
- w_gate: bfloat16 [960, 2560], P('row', 'col'), may hold values from -0.1875 to 0.1875
- w_up: bfloat16 [960, 2560], P('row', 'col'), may hold values from -0.1875 to 0.1875
- w_down: bfloat16 [2560, 960], P('row', 'col'), may hold values from -0.125 to 0.125
- cotangent: bfloat16 [32, 512, 960], P(('row', 'col')), may hold values from -6 to 6
Outputs:
- output: bfloat16 [32, 512, 960], P(('row', 'col'))
- token_grad: bfloat16 [32, 512, 960], P(('row', 'col'))
- attn_gain_grad: float32 [960], P('row')
- router_grad: float32 [960, 3], P('row')
- w_query_grad: float32 [960, 960], P('row', 'col')
- w_key_grad: float32 [960, 320], P('row', 'col')
- w_value_grad: float32 [960, 320], P('row', 'col')
- w_out_grad: float32 [960, 960], P('row', 'col')
- ffn_gain_grad: float32 [960], P('row')
- w_gate_grad: float32 [960, 2560], P('row', 'col')
- w_up_grad: float32 [960, 2560], P('row', 'col')
- w_down_grad: float32 [2560, 960], P('row', 'col')
Inputs may be any that keep to these rules, and one draw needn't show every extreme that they name: `segment_ids`: along a row the segment ids never fall; equal ids mark one document. `route_one`: each row holds 384 distinct positions of its sequence in ascending order. `route_two`: each row holds 256 distinct positions in ascending order, all in the same row of route_one. `route_three`: each row holds 128 distinct positions in ascending order, all in the same row of route_two.
All inputs are finite; a program needn't handle non-finite values.
Results may differ from a plain program's by a relative error of at most 0.028.
Values may be sent and summed in bfloat16 or wider, within the bound.
No kernel may reach another device: no remote copies, remote signals or barrier semaphores. Data moves between devices by JAX's collectives and lax.ppermute only.
A program may use at most 192 MiB of HBM per device.

v0:
```python
import jax
import jax.numpy as jnp
from jax import lax
from jax.sharding import PartitionSpec as P

HEADS = 15
KV_HEADS = 5
HEAD_DIM = 64
STEPS = 3


highest = lax.Precision.HIGHEST
eps_norm = 1e-05
rope_base = 10000.0


def rms_scale(values, gain_vec):
    return (
        values * lax.rsqrt(jnp.mean(values * values, axis=-1, keepdims=True) + eps_norm) * gain_vec
    )


def positions_of(segment_row):
    length = segment_row.shape[0]
    places = jnp.arange(length, dtype=jnp.int32)
    earlier = (segment_row[None, :] == segment_row[:, None]) & (places[None, :] < places[:, None])
    return jnp.sum(earlier.astype(jnp.int32), axis=1)


def rotary_tables(places):
    half_dim = HEAD_DIM // 2
    inverse = rope_base ** (-(jnp.arange(half_dim, dtype=jnp.float32) * 2.0 / HEAD_DIM))
    angles = places.astype(jnp.float32)[:, None] * inverse[None, :]
    return (jnp.cos(angles), jnp.sin(angles))


def rotate(values, cosine, sine_table):
    half_dim = values.shape[-1] // 2
    first_half = values[..., :half_dim]
    second = values[..., half_dim:]
    return jnp.concatenate(
        [first_half * cosine - second * sine_table, second * cosine + first_half * sine_table],
        axis=-1,
    )


def rotate_back(grads, cosine, sine_table):
    unused_value, pull_rotate = jax.vjp(lambda values: rotate(values, cosine, sine_table), grads)
    return pull_rotate(grads)[0]


def silu_product(gate_raw, up_raw):
    return jax.nn.silu(gate_raw) * up_raw


def step_parts(stream, chosen, segment_row, place_row, router_col, weight_set, kept_total):
    w_query, w_key, w_value, w_out, attn_gain, w_gate, w_up, w_down, ffn_gain = weight_set
    rows_picked = chosen.shape[0]
    groups = HEADS // KV_HEADS
    picked = jnp.take(stream, chosen, axis=0)
    gate_value = jax.nn.sigmoid(jnp.dot(picked, router_col, precision=highest))
    normed = rms_scale(picked, attn_gain.astype(jnp.float32)).astype(jnp.bfloat16)
    query_raw = jnp.dot(normed, w_query, preferred_element_type=jnp.float32).reshape(
        rows_picked, KV_HEADS, groups, HEAD_DIM
    )
    key_raw = jnp.dot(normed, w_key, preferred_element_type=jnp.float32).reshape(
        rows_picked, KV_HEADS, HEAD_DIM
    )
    value_heads = (
        jnp.dot(normed, w_value, preferred_element_type=jnp.float32)
        .astype(jnp.bfloat16)
        .reshape(rows_picked, KV_HEADS, HEAD_DIM)
    )
    cosine, sine_table = rotary_tables(jnp.take(place_row, chosen))
    query_rot = rotate(query_raw, cosine[:, None, None, :], sine_table[:, None, None, :]).astype(
        jnp.bfloat16
    )
    key_rot = rotate(key_raw, cosine[:, None, :], sine_table[:, None, :]).astype(jnp.bfloat16)
    segment_pick = jnp.take(segment_row, chosen)
    allowed = (segment_pick[None, :] == segment_pick[:, None]) & (
        chosen[None, :] <= chosen[:, None]
    )
    scores = jnp.einsum(
        "qkgd,skd->kgqs", query_rot, key_rot, preferred_element_type=jnp.float32
    ) * HEAD_DIM ** (-0.5)
    masked = jnp.where(allowed, scores, -1e30)
    if kept_total is None:
        row_max = jnp.max(masked, axis=-1, keepdims=True)
        log_total = row_max + jnp.log(jnp.sum(jnp.exp(masked - row_max), axis=-1, keepdims=True))
    else:
        log_total = kept_total
    prob_full = jnp.exp(masked - log_total)
    prob_low = prob_full.astype(jnp.bfloat16)
    mixed = jnp.einsum("kgqs,skd->qkgd", prob_low, value_heads, preferred_element_type=jnp.float32)
    mixed_low = mixed.reshape(rows_picked, HEADS * HEAD_DIM).astype(jnp.bfloat16)
    attn_out = jnp.dot(mixed_low, w_out, preferred_element_type=jnp.float32)
    middle = picked + attn_out
    normed_two = rms_scale(middle, ffn_gain.astype(jnp.float32)).astype(jnp.bfloat16)
    gate_raw = jnp.dot(normed_two, w_gate, preferred_element_type=jnp.float32)
    up_raw = jnp.dot(normed_two, w_up, preferred_element_type=jnp.float32)
    hidden = silu_product(gate_raw, up_raw).astype(jnp.bfloat16)
    ffn_out = jnp.dot(hidden, w_down, preferred_element_type=jnp.float32)
    return (
        picked,
        gate_value,
        normed,
        query_rot,
        key_rot,
        value_heads,
        log_total,
        prob_full,
        prob_low,
        mixed_low,
        attn_out,
        middle,
        normed_two,
        gate_raw,
        up_raw,
        hidden,
        ffn_out,
        cosine,
        sine_table,
    )


def step_forward(stream, chosen, segment_row, place_row, router_col, weight_set):
    parts = step_parts(stream, chosen, segment_row, place_row, router_col, weight_set, None)
    updated = parts[0] + parts[1][:, None] * (parts[10] + parts[16])
    return (stream.at[chosen].set(updated), parts[6])


def step_back(
    stream,
    grad_stream,
    chosen,
    segment_row,
    place_row,
    router_col,
    weight_set,
    kept_total,
    step_index,
):
    w_query, w_key, w_value, w_out, attn_gain, w_gate, w_up, w_down, ffn_gain = weight_set
    (
        picked,
        gate_value,
        normed,
        query_rot,
        key_rot,
        value_heads,
        log_total,
        prob_full,
        prob_low,
        mixed_low,
        attn_out,
        middle,
        normed_two,
        gate_raw,
        up_raw,
        hidden,
        ffn_out,
        cosine,
        sine_table,
    ) = step_parts(stream, chosen, segment_row, place_row, router_col, weight_set, kept_total)
    rows_picked = chosen.shape[0]
    groups = HEADS // KV_HEADS
    score_scale = HEAD_DIM ** (-0.5)
    grad_new = jnp.take(grad_stream, chosen, axis=0)
    grad_logit = jnp.sum(grad_new * (attn_out + ffn_out), axis=1) * gate_value * (1.0 - gate_value)
    grad_branch = gate_value[:, None] * grad_new
    grad_ffn = grad_branch.astype(jnp.bfloat16)
    grad_down_w = jnp.einsum("ch,cd->hd", hidden, grad_ffn, preferred_element_type=jnp.float32)
    grad_hidden = jnp.einsum("cd,hd->ch", grad_ffn, w_down, preferred_element_type=jnp.float32)
    unused_hidden, pull_silu = jax.vjp(silu_product, gate_raw, up_raw)
    grad_gate_raw, grad_up_raw = pull_silu(grad_hidden)
    grad_gate_low = grad_gate_raw.astype(jnp.bfloat16)
    grad_up_low = grad_up_raw.astype(jnp.bfloat16)
    grad_gate_w = jnp.einsum(
        "cd,ch->dh", normed_two, grad_gate_low, preferred_element_type=jnp.float32
    )
    grad_up_w = jnp.einsum("cd,ch->dh", normed_two, grad_up_low, preferred_element_type=jnp.float32)
    grad_normed_two = jnp.einsum(
        "ch,dh->cd", grad_gate_low, w_gate, preferred_element_type=jnp.float32
    )
    grad_normed_two = grad_normed_two + jnp.einsum(
        "ch,dh->cd", grad_up_low, w_up, preferred_element_type=jnp.float32
    )
    unused_second, pull_two = jax.vjp(rms_scale, middle, ffn_gain.astype(jnp.float32))
    grad_middle, grad_ffn_gain = pull_two(grad_normed_two)
    grad_attn = (grad_branch + grad_middle).astype(jnp.bfloat16)
    grad_out_w = jnp.einsum("ce,cd->ed", mixed_low, grad_attn, preferred_element_type=jnp.float32)
    grad_mixed = jnp.einsum("cd,ed->ce", grad_attn, w_out, preferred_element_type=jnp.float32)
    grad_mixed = grad_mixed.astype(jnp.bfloat16).reshape(rows_picked, KV_HEADS, groups, HEAD_DIM)
    grad_prob = jnp.einsum(
        "qkgd,skd->kgqs", grad_mixed, value_heads, preferred_element_type=jnp.float32
    )
    grad_value = jnp.einsum(
        "kgqs,qkgd->skd", prob_low, grad_mixed, preferred_element_type=jnp.float32
    )
    grad_value = grad_value.reshape(rows_picked, KV_HEADS * HEAD_DIM).astype(jnp.bfloat16)
    row_dot = jnp.sum(prob_full * grad_prob, axis=-1, keepdims=True)
    grad_scores = (prob_full * (grad_prob - row_dot)).astype(jnp.bfloat16)
    grad_query_rot = (
        jnp.einsum("kgqs,skd->qkgd", grad_scores, key_rot, preferred_element_type=jnp.float32)
        * score_scale
    )
    grad_key_rot = (
        jnp.einsum("kgqs,qkgd->skd", grad_scores, query_rot, preferred_element_type=jnp.float32)
        * score_scale
    )
    grad_query = rotate_back(grad_query_rot, cosine[:, None, None, :], sine_table[:, None, None, :])
    grad_query = grad_query.reshape(rows_picked, HEADS * HEAD_DIM).astype(jnp.bfloat16)
    grad_key = rotate_back(grad_key_rot, cosine[:, None, :], sine_table[:, None, :])
    grad_key = grad_key.reshape(rows_picked, KV_HEADS * HEAD_DIM).astype(jnp.bfloat16)
    grad_query_w = jnp.einsum("cd,ce->de", normed, grad_query, preferred_element_type=jnp.float32)
    grad_key_w = jnp.einsum("cd,ce->de", normed, grad_key, preferred_element_type=jnp.float32)
    grad_value_w = jnp.einsum("cd,ce->de", normed, grad_value, preferred_element_type=jnp.float32)
    grad_normed = jnp.einsum("ce,de->cd", grad_query, w_query, preferred_element_type=jnp.float32)
    grad_normed = grad_normed + jnp.einsum(
        "ce,de->cd", grad_key, w_key, preferred_element_type=jnp.float32
    )
    grad_normed = grad_normed + jnp.einsum(
        "ce,de->cd", grad_value, w_value, preferred_element_type=jnp.float32
    )
    unused_first, pull_one = jax.vjp(rms_scale, picked, attn_gain.astype(jnp.float32))
    grad_norm, grad_attn_gain = pull_one(grad_normed)
    grad_picked = grad_new + grad_middle + grad_norm + grad_logit[:, None] * router_col[None, :]
    grad_router_col = jnp.dot(grad_logit, picked, precision=highest)
    step_mask = (jnp.arange(STEPS) == step_index).astype(jnp.float32)
    grad_router = grad_router_col[:, None] * step_mask[None, :]
    step_grads = (
        grad_query_w,
        grad_key_w,
        grad_value_w,
        grad_out_w,
        grad_attn_gain,
        grad_router,
        grad_gate_w,
        grad_up_w,
        grad_down_w,
        grad_ffn_gain,
    )
    return (grad_stream.at[chosen].set(grad_picked), step_grads)


def body(
    tokens,
    segment_ids,
    route_one,
    route_two,
    route_three,
    attn_gain,
    router,
    w_query,
    w_key,
    w_value,
    w_out,
    ffn_gain,
    w_gate,
    w_up,
    w_down,
    cotangent,
):
    col_count = lax.axis_size("col")
    query_rows, key_rows, value_rows, out_rows, attn_gain_rows, router_rows = (
        lax.all_gather(w_query, "row", axis=0, tiled=True),
        lax.all_gather(w_key, "row", axis=0, tiled=True),
        lax.all_gather(w_value, "row", axis=0, tiled=True),
        lax.all_gather(w_out, "row", axis=0, tiled=True),
        lax.all_gather(attn_gain.reshape(-1, 1), "row", axis=0, tiled=True),
        lax.all_gather(router, "row", axis=0, tiled=True),
    )
    full_query, full_key, full_value, full_out = (
        lax.all_gather(query_rows, "col", axis=1, tiled=True),
        lax.all_gather(key_rows, "col", axis=1, tiled=True),
        lax.all_gather(value_rows, "col", axis=1, tiled=True),
        lax.all_gather(out_rows, "col", axis=1, tiled=True),
    )
    full_attn_gain = attn_gain_rows[:, 0]
    gate_rows, up_rows, down_rows, ffn_gain_rows = (
        lax.all_gather(w_gate, "row", axis=0, tiled=True),
        lax.all_gather(w_up, "row", axis=0, tiled=True),
        lax.all_gather(w_down, "row", axis=0, tiled=True),
        lax.all_gather(ffn_gain.reshape(-1, 1), "row", axis=0, tiled=True),
    )
    full_gate, full_up, full_down = (
        lax.all_gather(gate_rows, "col", axis=1, tiled=True),
        lax.all_gather(up_rows, "col", axis=1, tiled=True),
        lax.all_gather(down_rows, "col", axis=1, tiled=True),
    )
    full_ffn_gain = ffn_gain_rows[:, 0]
    weight_set = (
        full_query,
        full_key,
        full_value,
        full_out,
        full_attn_gain,
        full_gate,
        full_up,
        full_down,
        full_ffn_gain,
    )
    router_cols = router_rows.astype(jnp.float32)
    totals = None
    segment_row = segment_ids[0]
    place_row = positions_of(segment_row)
    routes = (route_one[0], route_two[0], route_three[0])
    stream = tokens[0].astype(jnp.float32)
    kept_streams = []
    kept_totals = []
    for step_index in range(STEPS):
        kept_streams.append(stream)
        stream, log_total = step_forward(
            stream,
            routes[step_index],
            segment_row,
            place_row,
            router_cols[:, step_index],
            weight_set,
        )
        kept_totals.append(log_total)
    outputs = [stream.astype(jnp.bfloat16)]
    grad_stream = cotangent[0].astype(jnp.float32)
    for step_index in reversed(range(STEPS)):
        grad_stream, step_grads = step_back(
            kept_streams[step_index],
            grad_stream,
            routes[step_index],
            segment_row,
            place_row,
            router_cols[:, step_index],
            weight_set,
            kept_totals[step_index],
            step_index,
        )
        totals = step_grads if totals is None else jax.tree.map(jnp.add, totals, step_grads)
    token_grads = [grad_stream.astype(jnp.bfloat16)]
    (
        grad_query_w,
        grad_key_w,
        grad_value_w,
        grad_out_w,
        grad_attn_gain,
        grad_router,
        grad_gate_w,
        grad_up_w,
        grad_down_w,
        grad_ffn_gain,
    ) = totals
    attn_gain_wide = jnp.tile(grad_attn_gain[:, None], (1, col_count))
    router_wide = jnp.tile(grad_router, (1, col_count))
    ffn_gain_wide = jnp.tile(grad_ffn_gain[:, None], (1, col_count))
    query_cols, key_cols, value_cols, out_cols, attn_gain_cols, router_part = (
        lax.psum_scatter(
            grad_query_w.astype(jnp.bfloat16), "col", scatter_dimension=1, tiled=True
        ).astype(jnp.float32),
        lax.psum_scatter(
            grad_key_w.astype(jnp.bfloat16), "col", scatter_dimension=1, tiled=True
        ).astype(jnp.float32),
        lax.psum_scatter(
            grad_value_w.astype(jnp.bfloat16), "col", scatter_dimension=1, tiled=True
        ).astype(jnp.float32),
        lax.psum_scatter(
            grad_out_w.astype(jnp.bfloat16), "col", scatter_dimension=1, tiled=True
        ).astype(jnp.float32),
        lax.psum_scatter(
            attn_gain_wide.astype(jnp.bfloat16), "col", scatter_dimension=1, tiled=True
        ).astype(jnp.float32),
        lax.psum_scatter(
            router_wide.astype(jnp.bfloat16), "col", scatter_dimension=1, tiled=True
        ).astype(jnp.float32),
    )
    query_block, key_block, value_block, out_block, attn_gain_block, router_block = (
        lax.psum_scatter(
            query_cols.astype(jnp.bfloat16), "row", scatter_dimension=0, tiled=True
        ).astype(jnp.float32),
        lax.psum_scatter(
            key_cols.astype(jnp.bfloat16), "row", scatter_dimension=0, tiled=True
        ).astype(jnp.float32),
        lax.psum_scatter(
            value_cols.astype(jnp.bfloat16), "row", scatter_dimension=0, tiled=True
        ).astype(jnp.float32),
        lax.psum_scatter(
            out_cols.astype(jnp.bfloat16), "row", scatter_dimension=0, tiled=True
        ).astype(jnp.float32),
        lax.psum_scatter(
            attn_gain_cols.astype(jnp.bfloat16), "row", scatter_dimension=0, tiled=True
        ).astype(jnp.float32),
        lax.psum_scatter(
            router_part.astype(jnp.bfloat16), "row", scatter_dimension=0, tiled=True
        ).astype(jnp.float32),
    )
    gate_cols, up_cols, down_cols, ffn_gain_cols = (
        lax.psum_scatter(
            grad_gate_w.astype(jnp.bfloat16), "col", scatter_dimension=1, tiled=True
        ).astype(jnp.float32),
        lax.psum_scatter(
            grad_up_w.astype(jnp.bfloat16), "col", scatter_dimension=1, tiled=True
        ).astype(jnp.float32),
        lax.psum_scatter(
            grad_down_w.astype(jnp.bfloat16), "col", scatter_dimension=1, tiled=True
        ).astype(jnp.float32),
        lax.psum_scatter(
            ffn_gain_wide.astype(jnp.bfloat16), "col", scatter_dimension=1, tiled=True
        ).astype(jnp.float32),
    )
    gate_block, up_block, down_block, ffn_gain_block = (
        lax.psum_scatter(
            gate_cols.astype(jnp.bfloat16), "row", scatter_dimension=0, tiled=True
        ).astype(jnp.float32),
        lax.psum_scatter(
            up_cols.astype(jnp.bfloat16), "row", scatter_dimension=0, tiled=True
        ).astype(jnp.float32),
        lax.psum_scatter(
            down_cols.astype(jnp.bfloat16), "row", scatter_dimension=0, tiled=True
        ).astype(jnp.float32),
        lax.psum_scatter(
            ffn_gain_cols.astype(jnp.bfloat16), "row", scatter_dimension=0, tiled=True
        ).astype(jnp.float32),
    )
    return (
        jnp.stack(outputs),
        jnp.stack(token_grads),
        attn_gain_block[:, 0],
        router_block,
        query_block,
        key_block,
        value_block,
        out_block,
        ffn_gain_block[:, 0],
        gate_block,
        up_block,
        down_block,
    )


def solution(mesh):
    return jax.shard_map(
        body,
        mesh=mesh,
        in_specs=(
            P(("row", "col"), None, None),
            P(("row", "col"), None),
            P(("row", "col"), None),
            P(("row", "col"), None),
            P(("row", "col"), None),
            P("row"),
            P("row", None),
            P("row", "col"),
            P("row", "col"),
            P("row", "col"),
            P("row", "col"),
            P("row"),
            P("row", "col"),
            P("row", "col"),
            P("row", "col"),
            P(("row", "col"), None, None),
        ),
        out_specs=(
            P(("row", "col"), None, None),
            P(("row", "col"), None, None),
            P("row"),
            P("row", None),
            P("row", "col"),
            P("row", "col"),
            P("row", "col"),
            P("row", "col"),
            P("row"),
            P("row", "col"),
            P("row", "col"),
            P("row", "col"),
        ),
        check_vma=False,
    )
```

profile of v0, /device:TPU:0, one launch (start us, length us, event | category | flops | bytes accessed | tf_op | source)
XLA Modules:
  0.0 961.5 jit_solution(11797903330112536966)
XLA Ops:
  7.2 10.9 %all_gather.57 = bf16[960,120]{1,0:T(8,128)(2,1)S(1)} all-gather(bf16[240,120]{1,0:T(8,128)(2,1)} %param.35), channel_id=1, replica_groups=mesh['row'=4,'col'=8] {'row'}, dimensions={0}, use_global_device_ids=true | all-gather | bytes 288000 | tf_op jit(solution)/shard_map/all_gather | solution.py:266
  19.0 8.7 all_gather.59
  28.6 10.0 %all-gather.5 = bf16[4,240,320]{1,2,0:T(8,128)(2,1)S(1)} all-gather(bf16[1,240,320]{1,2,0:T(8,128)(2,1)S(1)} %bitcast.452), channel_id=1, replica_groups=mesh['row'=4,'col'=8] {'row'}, dimensions={0}, use_global_device_ids=true | all-gather | bytes 768000 | tf_op jit(solution)/shard_map/all_gather | solution.py:281
  40.6 11.2 %all-gather.6 = bf16[4,240,320]{1,2,0:T(8,128)(2,1)S(1)} all-gather(bf16[1,240,320]{1,2,0:T(8,128)(2,1)S(1)} %bitcast.453), channel_id=1, replica_groups=mesh['row'=4,'col'=8] {'row'}, dimensions={0}, use_global_device_ids=true | all-gather | bytes 768000 | tf_op jit(solution)/shard_map/all_gather | solution.py:282
  53.8 10.7 %all_gather.66 = bf16[2560,120]{0,1:T(8,128)(2,1)} all-gather(bf16[640,120]{0,1:T(8,128)(2,1)S(1)} %copy-done.147), channel_id=1, replica_groups=mesh['row'=4,'col'=8] {'row'}, dimensions={0}, use_global_device_ids=true | all-gather | bytes 768000 | tf_op jit(solution)/shard_map/all_gather | solution.py:283
  75.4 2.8 gather_fusion.1
  80.7 3.0 copy.154
  83.7 7.9 all-gather.2
  97.2 2.8 bitcast_convert_fusion
  100.1 2.8 gather_fusion.2
  102.9 7.5 all-gather.3
  112.4 8.9 all-reduce.28
  121.3 8.2 all-gather.4
  136.9 17.7 %all_gather.56 = bf16[960,320]{0,1:T(8,128)(2,1)S(1)} all-gather(bf16[960,40]{0,1:T(8,128)(2,1)S(1)} %reshape.979), channel_id=1, replica_groups=mesh['row'=4,'col'=8] {'col'}, dimensions={1}, use_global_device_ids=true | all-gather | bytes 691200 | tf_op jit(solution)/shard_map/all_gather | solution.py:275
  157.0 19.1 %all_gather.54 = bf16[960,320]{0,1:T(8,128)(2,1)S(1)} all-gather(bf16[960,40]{0,1:T(8,128)(2,1)S(1)} %reshape.977), channel_id=1, replica_groups=mesh['row'=4,'col'=8] {'col'}, dimensions={1}, use_global_device_ids=true | all-gather | bytes 691200 | tf_op jit(solution)/shard_map/all_gather | solution.py:276
  178.2 2.8 fusion.154
  188.6 4.5 multiply_reduce_fusion.5
  194.5 7.0 fusion.129
  201.4 9.0 multiply_convert_fusion.1
  210.4 41.4 %all-gather.21.cloned.1.call-done = bf16[2560,960]{0,1:T(8,128)(2,1)} async-done(((bf16[2560,120]{0,1:T(8,128)(2,1)}), bf16[2560,960]{0,1:T(8,128)(2,1)}) %all-gather.21.cloned.1.call-update) | async-done | bytes 4915216 | tf_op jit(solution)/shard_map/all_gather | solution.py:289
  251.8 8.2 multiply_add_fusion
  260.0 3.0 copy.163
  263.0 3.6 scatter_fusion
  283.8 3.7 multiply_convert_fusion.3
  287.6 2.7 multiply_add_fusion.1
  292.9 3.4 scatter_fusion.1
  308.1 5.2 fusion.131
  340.4 6.7 multiply_convert_fusion.2
  347.2 5.6 fusion.136
  352.9 5.5 multiply_reduce_fusion.7
  366.0 3.0 fusion.141
  381.3 3.0 scatter_fusion.4
  386.8 3.0 copy.181
  389.8 8.9 multiply_convert_fusion
  398.8 6.7 fusion.138
  405.5 6.4 multiply_reduce_fusion
  415.4 3.0 fusion
  429.2 3.8 copy.216
  439.1 3.8 copy.222
  444.1 2.9 fusion.78
  447.1 5.3 fusion.76
  452.4 7.9 add_convert_fusion.2
  461.5 3.8 fusion.32
  468.7 6.6 fusion.34
  478.5 7.2 fusion.150
  485.8 7.0 fusion.149
  492.8 8.3 add_convert_fusion.1
  501.6 6.7 fusion.151
  508.3 2.9 fusion.152
  511.2 8.3 add_convert_fusion
  535.6 25.8 %reduce-scatter.36.cloned.1.call-done = bf16[2560,120]{0,1:T(8,128)(2,1)} async-done(((bf16[2560,960]{0,1:T(8,128)(2,1)}), bf16[2560,120]{0,1:T(8,128)(2,1)}) %reduce-scatter.36.cloned.1.call-update) | async-done | bytes 614416 | tf_op jit(solution)/shard_map/reduce_scatter | solution.py:400
  571.5 23.1 %reduce-scatter.28.cloned.1.call-done = bf16[960,40]{0,1:T(8,128)(2,1)} async-done(((bf16[960,320]{0,1:T(8,128)(2,1)}), bf16[960,40]{0,1:T(8,128)(2,1)}) %reduce-scatter.28.cloned.1.call-update) | async-done | bytes 76816 | tf_op jit(solution)/shard_map/reduce_scatter | solution.py:357
  594.6 31.8 %reduce-scatter.30.cloned.1.call-done = bf16[960,40]{0,1:T(8,128)(2,1)} async-done(((bf16[960,320]{0,1:T(8,128)(2,1)}), bf16[960,40]{0,1:T(8,128)(2,1)}) %reduce-scatter.30.cloned.1.call-update) | async-done | bytes 76816 | tf_op jit(solution)/shard_map/reduce_scatter | solution.py:360
  626.4 60.4 %reduce-scatter.32.cloned.1.call-done = bf16[960,320]{0,1:T(8,128)(2,1)} async-done(((bf16[960,2560]{0,1:T(8,128)(2,1)}), bf16[960,320]{0,1:T(8,128)(2,1)}) %reduce-scatter.32.cloned.1.call-update) | async-done | bytes 614416 | tf_op jit(solution)/shard_map/reduce_scatter | solution.py:394
  686.8 60.5 %reduce-scatter.34.cloned.1.call-done = bf16[960,320]{0,1:T(8,128)(2,1)} async-done(((bf16[960,2560]{0,1:T(8,128)(2,1)}), bf16[960,320]{0,1:T(8,128)(2,1)}) %reduce-scatter.34.cloned.1.call-update) | async-done | bytes 614416 | tf_op jit(solution)/shard_map/reduce_scatter | solution.py:397
  747.4 3.6 fusion.18
  751.0 3.1 copy.185
  754.1 3.6 scatter_fusion.5
  759.2 40.5 %all-reduce.33.cloned.1.call-done = (bf16[960,8]{0,1:T(8,128)(2,1)}, bf16[960,24]{0,1:T(8,128)(2,1)}, bf16[960,8]{0,1:T(8,128)(2,1)}) async-done(((bf16[960,8]{0,1:T(8,128)(2,1)}, bf16[960,24]{0,1:T(8,128)(2,1)}, bf16[960,8]{0,1:T(8,128)(2,1)}), (bf16[960,8]{0,1:T(8,128)(2,1)}, bf16[960,24]{0,1:T(8,128)(2,1)}, bf16[960,8]{0,1:T(8,128)(2,1)})) %all-reduce.33.cloned.1.call-update) | async-done | bytes 76816
  803.3 16.1 %all-reduce.27 = (bf16[960,1]{0,1:T(2,128)(2,1)S(1)}, bf16[960,3]{0,1:T(4,128)(2,1)S(1)}, bf16[960,1]{0,1:T(2,128)(2,1)S(1)}) all-reduce(bf16[960,1]{0,1:T(2,128)(2,1)S(1)} %constant_dynamic-slice_fusion.5, bf16[960,3]{0,1:T(4,128)(2,1)S(1)} %constant_dynamic-slice_fusion.3, ...), channel_id=5, replica_groups=mesh['row'=4,'col'=8] {'row'}, use_global_device_ids=true, to_apply=%region_35.42.clone | all-reduce | flops 4800 | bytes 19200
  821.3 8.8 reduce-scatter.44.cloned.1.call-done
  831.6 25.5 %reduce-scatter.46.cloned.1.call-done = bf16[240,120]{1,0:T(8,128)(2,1)} async-done(((bf16[960,120]{1,0:T(8,128)(2,1)}), bf16[240,120]{1,0:T(8,128)(2,1)}) %reduce-scatter.46.cloned.1.call-update) | async-done | bytes 57616
  858.6 26.9 %reduce-scatter.42.cloned.1.call-done = bf16[640,120]{1,0:T(8,128)(2,1)} async-done(((bf16[2560,120]{1,0:T(8,128)(2,1)}), bf16[640,120]{1,0:T(8,128)(2,1)}) %reduce-scatter.42.cloned.1.call-update) | async-done | bytes 153616
  887.3 61.0 %all-reduce.35.cloned.1.call-done = (bf16[960,40]{0,1:T(8,128)(2,1)}, bf16[960,40]{0,1:T(8,128)(2,1)}, bf16[960,320]{0,1:T(8,128)(2,1)}, bf16[960,320]{0,1:T(8,128)(2,1)}) async-done(((bf16[960,40]{0,1:T(8,128)(2,1)}, bf16[960,40]{0,1:T(8,128)(2,1)}, bf16[960,320]{0,1:T(8,128)(2,1)}, bf16[960,320]{0,1:T(8,128)(2,1)}), (bf16[960,40]{0,1:T(8,128)(2,1)}, bf16[960,40]{0,1:T(8,128)(2,1)}, ...) | async-done | bytes 1382416
  (739 shorter events, 198.2 us)
Async XLA Ops:
  7.2 21.4 %copy-start.145 = (bf16[240,320]{0,1:T(8,128)(2,1)S(1)}, bf16[240,320]{0,1:T(8,128)(2,1)}, u32[]{:S(2)}) copy-start(bf16[240,320]{0,1:T(8,128)(2,1)} %param.40) | copy-start | bytes 460804
  7.2 171.0 %all-gather.13.cloned.1.call-start = ((), (), s32[]{:S(2)}) async-start(), calls=%async_computation.10 | async-start | bytes 2211840 | tf_op jit(solution)/shard_map/all_gather | solution.py:274
  19.0 169.6 %all-gather.15.cloned.1.call-start = ((), (), s32[]{:S(2)}) async-start(), calls=%async_computation.11 | async-start | bytes 2211840 | tf_op jit(solution)/shard_map/all_gather | solution.py:277
  28.6 165.9 %all-gather.17.cloned.1.call-start = ((), (), s32[]{:S(2)}) async-start(), calls=%async_computation.12 | async-start | bytes 5898240 | tf_op jit(solution)/shard_map/all_gather | solution.py:287
  28.6 12.0 %copy-start.146 = (bf16[240,320]{0,1:T(8,128)(2,1)S(1)}, bf16[240,320]{0,1:T(8,128)(2,1)}, u32[]{:S(2)}) copy-start(bf16[240,320]{0,1:T(8,128)(2,1)} %param.41) | copy-start | bytes 460804
  40.6 160.9 %all-gather.19.cloned.1.call-start = ((), (), s32[]{:S(2)}) async-start(), calls=%async_computation.13 | async-start | bytes 5898240 | tf_op jit(solution)/shard_map/all_gather | solution.py:288
  40.6 13.2 %copy-start.147 = (bf16[640,120]{0,1:T(8,128)(2,1)S(1)}, bf16[640,120]{0,1:T(8,128)(2,1)}, u32[]{:S(2)}) copy-start(bf16[640,120]{0,1:T(8,128)(2,1)} %param.42) | copy-start | bytes 460804
  52.3 12.3 %copy-start.212 = (s32[1,128]{1,0:T(1,128)S(1)}, s32[1,128]{1,0:T(1,128)}, u32[]{:S(2)}) copy-start(s32[1,128]{1,0:T(1,128)} %param.32) | copy-start | bytes 1540
  52.3 12.9 %copy-start = (s32[1,512]{1,0:T(1,128)S(1)}, s32[1,512]{1,0:T(1,128)}, u32[]{:S(2)}) copy-start(s32[1,512]{1,0:T(1,128)} %param.29) | copy-start | bytes 6148
  52.3 13.1 %copy-start.172 = (s32[1,256]{1,0:T(1,128)S(1)}, s32[1,256]{1,0:T(1,128)}, u32[]{:S(2)}) copy-start(s32[1,256]{1,0:T(1,128)} %param.31) | copy-start | bytes 3076
  53.7 198.0 %all-gather.21.cloned.1.call-start = ((), (), s32[]{:S(2)}) async-start(), calls=%async_computation.14 | async-start | bytes 5529600 | tf_op jit(solution)/shard_map/all_gather | solution.py:289
  64.5 8.0 copy-start.108
  64.5 467.2 %reduce-scatter.38.cloned.1.call-start = ((), (), s32[]{:S(2)}) async-start(), calls=%async_computation.20 | async-start | bytes 2211840
  66.0 200.6 %copy-start.196 = (s32[1024]{0:T(1024)}, s32[1024]{0:T(1024)S(1)}, u32[]{:S(2)}) copy-start(s32[1024]{0:T(1024)S(1)} %pad_clamp_fusion.1) | copy-start | bytes 12292
  69.9 59.7 %copy-start.204 = (s32[1024]{0:T(1024)}, s32[1024]{0:T(1024)S(1)}, u32[]{:S(2)}) copy-start(s32[1024]{0:T(1024)S(1)} %pad_clamp_fusion) | copy-start | bytes 12292
  75.3 187.6 %copy-start.185 = (s32[384]{0:T(512)}, s32[384]{0:T(512)S(1)}, u32[]{:S(2)}) copy-start(s32[384]{0:T(512)S(1)} %fusion.91) | copy-start | bytes 4612
  75.4 24.7 %copy-start.160 = (s32[1024]{0:T(1024)}, s32[1024]{0:T(1024)S(1)}, u32[]{:S(2)}) copy-start(s32[1024]{0:T(1024)S(1)} %pad_clamp_fusion.2) | copy-start | bytes 12292
  83.7 168.1 %copy-start.152 = (pred[384]{0:T(512)(128)(4,1)}, pred[384]{0:T(512)(128)(4,1)S(1)}, u32[]{:S(2)}) copy-start(pred[384]{0:T(512)(128)(4,1)S(1)} %get-tuple-element.116) | copy-start | bytes 1156
  91.7 178.4 %copy-start.141 = (bf16[960,3]{0,1:T(4,128)(2,1)}, bf16[960,3]{0,1:T(4,128)(2,1)S(1)}, u32[]{:S(2)}) copy-start(bf16[960,3]{0,1:T(4,128)(2,1)S(1)} %reshape.975) | copy-start | bytes 17284
  94.8 156.9 %copy-start.165 = (f32[384]{0:T(512)}, f32[384]{0:T(512)S(1)}, u32[]{:S(2)}) copy-start(f32[384]{0:T(512)S(1)} %add_divide_fusion.3) | copy-start | bytes 4612
  94.9 59.7 %copy-start.168 = (f32[384]{0:T(512)}, f32[384]{0:T(512)S(1)}, u32[]{:S(2)}) copy-start(f32[384]{0:T(512)S(1)} %fusion.89) | copy-start | bytes 4612
  94.9 175.9 %copy-start.148 = (pred[256]{0:T(512)(128)(4,1)}, pred[256]{0:T(512)(128)(4,1)S(1)}, u32[]{:S(2)}) copy-start(pred[256]{0:T(512)(128)(4,1)S(1)} %get-tuple-element.112) | copy-start | bytes 772
  100.0 10.6 %copy-start.218 = (u32[32]{0:T(128)S(1)}, u32[32]{0:T(128)}, u32[]{:S(2)}) copy-start(u32[32]{0:T(128)} %constant.172) | copy-start | bytes 388
  100.0 11.9 %copy-start.219 = (bf16[240]{0:T(256)(128)(2,1)S(1)}, bf16[240]{0:T(256)(128)(2,1)}, u32[]{:S(2)}) copy-start(bf16[240]{0:T(256)(128)(2,1)} %param.33) | copy-start | bytes 1444
  100.0 12.2 %copy-start.220 = (bf16[240]{0:T(256)(128)(2,1)S(1)}, bf16[240]{0:T(256)(128)(2,1)}, u32[]{:S(2)}) copy-start(bf16[240]{0:T(256)(128)(2,1)} %param.39) | copy-start | bytes 1444
  100.0 21.3 %copy-start.176 = (bf16[240,40]{0,1:T(8,128)(2,1)S(1)}, bf16[240,40]{0,1:T(8,128)(2,1)}, u32[]{:S(2)}) copy-start(bf16[240,40]{0,1:T(8,128)(2,1)} %param.36) | copy-start | bytes 57604
  121.3 149.5 %copy-start.132 = (f32[960]{0:T(1024)}, f32[960]{0:T(1024)S(1)}, u32[]{:S(2)}) copy-start(f32[960]{0:T(1024)S(1)} %convert_element_type.498) | copy-start | bytes 11524
  129.7 63.5 %copy-start.119 = (f32[960]{0:T(1024)}, f32[960]{0:T(1024)S(1)}, u32[]{:S(2)}) copy-start(f32[960]{0:T(1024)S(1)} %convert_element_type.499) | copy-start | bytes 11524
  136.6 44.3 %copy-start.104 = (f32[384,32]{0,1:T(8,128)}, f32[384,32]{0,1:T(8,128)S(1)}, u32[]{:S(2)}) copy-start(f32[384,32]{0,1:T(8,128)S(1)} %get-tuple-element.152) | copy-start | bytes 147460
  136.7 44.3 %copy-start.106 = (f32[384,32]{0,1:T(8,128)}, f32[384,32]{0,1:T(8,128)S(1)}, u32[]{:S(2)}) copy-start(f32[384,32]{0,1:T(8,128)S(1)} %get-tuple-element.153) | copy-start | bytes 147460
  136.9 47.8 %copy-start.77 = (pred[384,384]{0,1:T(8,128)(4,1)}, pred[384,384]{0,1:T(8,128)(4,1)S(1)}, u32[]{:S(2)}) copy-start(pred[384,384]{0,1:T(8,128)(4,1)S(1)} %compare_and_fusion) | copy-start | bytes 442372
  156.4 21.8 %copy-start.38 = (bf16[384,960]{0,1:T(8,128)(2,1)}, bf16[384,960]{0,1:T(8,128)(2,1)S(1)}, u32[]{:S(2)}) copy-start(bf16[384,960]{0,1:T(8,128)(2,1)S(1)} %multiply_convert_fusion.5) | copy-start | bytes 2211844
  157.0 24.2 %copy-start.126 = (bf16[384,5,32]{0,2,1:T(8,128)(2,1)}, bf16[384,5,32]{0,2,1:T(8,128)(2,1)S(1)}, u32[]{:S(2)}) copy-start(bf16[384,5,32]{0,2,1:T(8,128)(2,1)S(1)} %get-tuple-element.135) | copy-start | bytes 368644
  157.0 24.2 %copy-start.128 = (bf16[384,5,32]{0,2,1:T(8,128)(2,1)}, bf16[384,5,32]{0,2,1:T(8,128)(2,1)S(1)}, u32[]{:S(2)}) copy-start(bf16[384,5,32]{0,2,1:T(8,128)(2,1)S(1)} %get-tuple-element.136) | copy-start | bytes 368644
  193.1 8.3 copy-start.183
  193.1 8.3 copy-start.162
  273.6 13.9 %copy-start.173 = (f32[256]{0:T(256)}, f32[256]{0:T(256)S(1)}, u32[]{:S(2)}) copy-start(f32[256]{0:T(256)S(1)} %add_divide_fusion.4) | copy-start | bytes 3076
  302.6 63.2 %copy-start.53 = (bf16[128,960]{0,1:T(8,128)(2,1)}, bf16[128,960]{0,1:T(8,128)(2,1)S(1)}, u32[]{:S(2)}) copy-start(bf16[128,960]{0,1:T(8,128)(2,1)S(1)} %multiply_convert_fusion.14) | copy-start | bytes 737284
  304.9 24.7 %copy-start.198 = (f32[128]{0:T(128)}, f32[128]{0:T(128)S(1)}, u32[]{:S(2)}) copy-start(f32[128]{0:T(128)S(1)} %fusion.44) | copy-start | bytes 1540
  307.1 8.1 slice-start.13
  316.7 9.0 copy-start.75
  366.0 8.3 copy-start.101
  405.5 9.8 %slice-start = ((s8[8847360]{0:T(1024)(128)(4,1)}), s8[4194304]{0:T(1024)(128)(4,1)S(1)}, s32[]{:S(2)}) async-start(s8[8847360]{0:T(1024)(128)(4,1)} %bitcast.392), calls=%async_computation.27 | async-start | bytes 8388608
  405.5 9.8 %slice-start.1 = ((s8[8847360]{0:T(1024)(128)(4,1)}), s8[4194304]{0:T(1024)(128)(4,1)S(1)}, s32[]{:S(2)}) async-start(s8[8847360]{0:T(1024)(128)(4,1)} %bitcast.392), calls=%async_computation.28 | async-start | bytes 8388608
  433.1 100.5 %reduce-scatter.40.cloned.1.call-start = ((), (), s32[]{:S(2)}) async-start(), calls=%async_computation.21 | async-start | bytes 2211840
  442.9 118.5 %reduce-scatter.36.cloned.1.call-start = ((), (), s32[]{:S(2)}) async-start(), calls=%async_computation.19 | async-start | bytes 5529600 | tf_op jit(solution)/shard_map/reduce_scatter | solution.py:400
  460.4 134.2 %reduce-scatter.28.cloned.1.call-start = ((), (), s32[]{:S(2)}) async-start(), calls=%async_computation.15 | async-start | bytes 737280 | tf_op jit(solution)/shard_map/reduce_scatter | solution.py:357
  475.3 151.1 %reduce-scatter.30.cloned.1.call-start = ((), (), s32[]{:S(2)}) async-start(), calls=%async_computation.16 | async-start | bytes 737280 | tf_op jit(solution)/shard_map/reduce_scatter | solution.py:360
  485.7 201.1 %reduce-scatter.32.cloned.1.call-start = ((), (), s32[]{:S(2)}) async-start(), calls=%async_computation.17 | async-start | bytes 5898240 | tf_op jit(solution)/shard_map/reduce_scatter | solution.py:394
  501.1 246.2 %reduce-scatter.34.cloned.1.call-start = ((), (), s32[]{:S(2)}) async-start(), calls=%async_computation.18 | async-start | bytes 5898240 | tf_op jit(solution)/shard_map/reduce_scatter | solution.py:397
  519.6 280.2 %all-reduce.33.cloned.1.call-start = ((), (), s32[]{:S(2)}) async-start(), calls=%async_computation.25 | async-start | bytes 163840
  529.5 34.3 %copy-start.221 = (u32[32]{0:T(128)S(1)}, u32[32]{0:T(128)}, u32[]{:S(2)}) copy-start(u32[32]{0:T(128)} %constant.184) | copy-start | bytes 388
  529.5 36.2 %copy-start.93 = (f32[128,960]{0,1:T(8,128)S(1)}, f32[128,960]{0,1:T(8,128)}, u32[]{:S(2)}) copy-start(f32[128,960]{0,1:T(8,128)} %get-tuple-element.132) | copy-start | bytes 1474564
  531.6 298.4 %reduce-scatter.44.cloned.1.call-start = ((), (), s32[]{:S(2)}) async-start(), calls=%async_computation.23 | async-start | bytes 307200
  533.5 32.5 %copy-start.2 = (f32[512,960]{1,0:T(8,128)S(1)}, f32[512,960]{1,0:T(8,128)}, u32[]{:S(2)}) copy-start(f32[512,960]{1,0:T(8,128)} %copy-done.1) | copy-start | bytes 5898244
  533.5 32.5 %copy-start.216 = (s32[128]{0:T(128)S(1)}, s32[128]{0:T(128)}, u32[]{:S(2)}) copy-start(s32[128]{0:T(128)} %fusion.96) | copy-start | bytes 1540
  533.5 323.6 %reduce-scatter.46.cloned.1.call-start = ((), (), s32[]{:S(2)}) async-start(), calls=%async_computation.24 | async-start | bytes 307200
  535.6 350.0 %reduce-scatter.42.cloned.1.call-start = ((), (), s32[]{:S(2)}) async-start(), calls=%async_computation.22 | async-start | bytes 819200
  563.6 384.6 %all-reduce.35.cloned.1.call-start = ((), (), s32[]{:S(2)}) async-start(), calls=%async_computation.26 | async-start | bytes 2949120
  569.0 178.3 %copy-start.8 = (f32[384,960]{0,1:T(8,128)S(1)}, f32[384,960]{0,1:T(8,128)}, u32[]{:S(2)}) copy-start(f32[384,960]{0,1:T(8,128)} %copy.154) | copy-start | bytes 4423684
  569.0 178.3 %copy-start.19 = (f32[384,960]{0,1:T(8,128)S(1)}, f32[384,960]{0,1:T(8,128)}, u32[]{:S(2)}) copy-start(f32[384,960]{0,1:T(8,128)} %copy.181) | copy-start | bytes 4423684
  569.0 178.3 %copy-start.164 = (f32[384]{0:T(512)S(1)}, f32[384]{0:T(512)}, u32[]{:S(2)}) copy-start(f32[384]{0:T(512)} %copy-done.162) | copy-start | bytes 4612
  569.0 178.3 %copy-start.178 = (f32[384]{0:T(512)S(1)}, f32[384]{0:T(512)}, u32[]{:S(2)}) copy-start(f32[384]{0:T(512)} %copy-done.177) | copy-start | bytes 4612
  569.0 178.3 %copy-start.192 = (f32[960,1]{0,1:T(1,128)S(1)}, f32[960,1]{0,1:T(1,128)}, u32[]{:S(2)}) copy-start(f32[960,1]{0,1:T(1,128)} %get-tuple-element.149) | copy-start | bytes 11524
  (191 other events, 537.7 us)
Sparse Core Ops, SparseCore 0:
  19.1 28.2 all-gather.12
  49.6 27.4 all-gather.14
  79.4 55.3 all-gather.16
  136.8 61.6 all-gather.18
  200.0 51.7 all-gather.20
  433.2 34.5 reduce-scatter.37
  470.0 34.1 reduce-scatter.39
  506.5 54.8 reduce-scatter.35
  564.3 30.2 reduce-scatter.27
  596.7 29.6 reduce-scatter.29
  628.7 58.0 reduce-scatter.31
  688.9 58.2 reduce-scatter.33
  750.4 49.3 all-reduce.32
  802.9 27.0 reduce-scatter.43
  833.3 23.7 reduce-scatter.45
  859.8 25.6 reduce-scatter.41
  888.8 59.4 all-reduce.34
where the time goes:
time: 973 us; the launch traced here: 961 us
  waiting for transfers between devices  406 us (42%)
  matrix products  219 us (23%)
  blocking collectives  137 us (14%)
  local copies, waits for them, and re-layouts  134 us (14%)
  other arithmetic  44.7 us (5%)
  between operations  19.5 us (2%)
    unnamed x24, waiting for transfers between devices  163 us
    reduce_scatter x1, waiting for transfers between devices, body(): lax.psum_scatter(grad_up_w.astype(jnp.bfloat16), 'col', scatter_dimension...  60.5 us
    reduce_scatter x1, waiting for transfers between devices, body(): lax.psum_scatter(grad_gate_w.astype(jnp.bfloat16), 'col', scatter_dimensi...  60.4 us
    unnamed x500, local copies, waits for them, and re-layouts  59.2 us
    all_gather x1, waiting for transfers between devices, body(): lax.all_gather(down_rows, 'col', axis=1, tiled=True)  41.4 us
    reduce_scatter x1, waiting for transfers between devices, body(): lax.psum_scatter(grad_value_w.astype(jnp.bfloat16), 'col', scatter_dimens...  31.8 us
    reduce_scatter x1, waiting for transfers between devices, body(): lax.psum_scatter(grad_down_w.astype(jnp.bfloat16), 'col', scatter_dimensi...  25.8 us
    unnamed x2, blocking collectives  25 us
  transfers between devices with their start and end apart: 17, of which 11 were waited for; matrix products, arithmetic and copies ran while one was open for 21% of the time, Pallas kernels for 0%

commit v1 on v0

v1 whole, which is shorter than its diff:
```python
import jax
import jax.numpy as jnp
from jax import lax
from jax.sharding import PartitionSpec as P

HEADS = 15
KV_HEADS = 5
GROUPS = 3
HEAD_DIM = 64
STEPS = 3
EPS = 1e-05
ROPE_BASE = 10000.0
SCALE = HEAD_DIM ** (-0.5)
F32 = jnp.float32
BF16 = jnp.bfloat16
highest = lax.Precision.HIGHEST


def dot(a, b):
    return jnp.dot(a, b, preferred_element_type=F32)


def dot_nt(a, b):
    return lax.dot_general(a, b, (((1,), (1,)), ((), ())), preferred_element_type=F32)


def dot_tn(a, b):
    return lax.dot_general(a, b, (((0,), (0,)), ((), ())), preferred_element_type=F32)


def rms(values):
    return lax.rsqrt(jnp.mean(values * values, axis=-1, keepdims=True) + EPS)


def rms_back(values, inverse, gain, grad):
    scaled = grad * gain
    inner = jnp.mean(scaled * values, axis=-1, keepdims=True)
    return inverse * scaled - values * (inverse * inverse * inverse * inner)


def rotate(values, cosine, sine):
    half = HEAD_DIM // 2
    a, b = values[..., :half], values[..., half:]
    return jnp.concatenate([a * cosine - b * sine, b * cosine + a * sine], axis=-1)


def token_order(segment_row, routes):
    length = segment_row.shape[0]
    places = jnp.arange(length, dtype=jnp.int32)
    level = jnp.zeros((length,), jnp.int32)
    for route in routes:
        level = level + jnp.sum((route[:, None] == places[None, :]).astype(jnp.int32), axis=0)
    before = (level[:, None] > level[None, :]) | (
        (level[:, None] == level[None, :]) & (places[:, None] < places[None, :])
    )
    spot = jnp.sum(before.astype(jnp.int32), axis=0)
    earlier = (segment_row[:, None] == segment_row[None, :]) & (places[:, None] < places[None, :])
    place = jnp.sum(earlier.astype(jnp.int32), axis=0)
    chosen = spot[None, :] == places[:, None]
    zero = jnp.int32(0)
    pick = lambda v: jnp.sum(jnp.where(chosen, v[None, :], zero), axis=1)
    return chosen.astype(BF16), pick(places), pick(segment_row), pick(place)


def pack_small(attn_gain, router, ffn_gain, width):
    flat = jnp.concatenate([attn_gain[:, None], router, ffn_gain[:, None]], axis=1).reshape(-1)
    rows = -(-flat.shape[0] // width)
    rows = -(-rows // 8) * 8
    return jnp.pad(flat, (0, rows * width - flat.shape[0])).reshape(rows, width)


def fold(block):
    half = block.shape[0] // 2
    return jnp.concatenate([block[:half], block[half:]], axis=1)


def unfold(block):
    half = block.shape[1] // 2
    return jnp.concatenate([block[:, :half], block[:, half:]], axis=0)


def body(
    tokens, segment_ids, route_one, route_two, route_three, attn_gain, router,
    w_query, w_key, w_value, w_out, ffn_gain, w_gate, w_up, w_down, cotangent,
):
    nr, nc = lax.axis_size("row"), lax.axis_size("col")
    dr = w_query.shape[0]
    width = nr * dr
    qc, kc = w_query.shape[1], w_key.shape[1]
    fc = w_gate.shape[1]
    pairs = [(i, i ^ 1) for i in range(nc)]
    core = lax.axis_index("col") % 2

    att = fold(jnp.concatenate([w_query, w_key, w_value, w_out], axis=1))
    att_rows = att.shape[0]
    att = jnp.concatenate([att, pack_small(attn_gain, router, ffn_gain, att.shape[1])], axis=0)
    swapped = lax.ppermute(jnp.where(core == 0, w_up, w_gate), "col", pairs)
    gu = jnp.where(
        core == 0,
        jnp.concatenate([w_gate, swapped], axis=1),
        jnp.concatenate([swapped, w_up], axis=1),
    )
    dn = w_down.T
    att_all = lax.all_gather(att, ("col", "row"), axis=0)
    gu_all = lax.all_gather(gu, ("col", "row"), axis=0)
    dn_all = lax.all_gather(dn, ("row", "col"), axis=0)
    fw = 2 * fc
    gu_all = gu_all.reshape(nc // 2, 2, width, fw)
    dn_all = dn_all.reshape(nr, width, w_down.shape[0])
    att_all = att_all.reshape(nc, nr, *att.shape)
    small = att_all[0, :, att_rows:].reshape(nr, -1)[:, : 5 * dr].reshape(width, 5)
    small = small.astype(F32)
    gain_one, router_cols, gain_two = small[:, 0], small[:, 1:4], small[:, 4]
    aw = att_all[:, :, :att_rows].reshape(nc, nr, att_rows, 2, qc * 2 + kc * 2)
    aw = aw.transpose(1, 3, 2, 0, 4).reshape(width, nc, qc * 2 + kc * 2)
    full_query = aw[:, :, :qc].reshape(width, -1)
    full_key = aw[:, :, qc : qc + kc].reshape(width, -1)
    full_value = aw[:, :, qc + kc : qc + 2 * kc].reshape(width, -1)
    full_out = aw[:, :, qc + 2 * kc :].reshape(width, -1)

    routes = (route_one[0], route_two[0], route_three[0])
    counts = tuple(route.shape[0] for route in routes)
    chosen, where_at, segment, place = token_order(segment_ids[0], routes)
    stream = dot(chosen, tokens[0])
    grad_stream = dot(chosen, cotangent[0])
    half = HEAD_DIM // 2
    inverse = ROPE_BASE ** (-(jnp.arange(half, dtype=F32) * 2.0 / HEAD_DIM))
    angles = place[: counts[0]].astype(F32)[:, None] * inverse[None, :]
    cosine, sine = jnp.cos(angles), jnp.sin(angles)
    top = counts[0]
    allowed = (segment[None, :top] == segment[:top, None]) & (
        where_at[None, :top] <= where_at[:top, None]
    )

    kept = []
    for step in range(STEPS):
        rows = counts[step]
        picked = stream[:rows]
        gate_value = jax.nn.sigmoid(jnp.dot(picked, router_cols[:, step], precision=highest))
        inv_one = rms(picked)
        normed = (picked * inv_one * gain_one).astype(BF16)
        co, si = cosine[:rows], sine[:rows]
        query = dot(normed, full_query).reshape(rows, KV_HEADS, GROUPS, HEAD_DIM)
        key = dot(normed, full_key).reshape(rows, KV_HEADS, HEAD_DIM)
        value = dot(normed, full_value).astype(BF16).reshape(rows, KV_HEADS, HEAD_DIM)
        query = rotate(query, co[:, None, None, :], si[:, None, None, :]).astype(BF16)
        key = rotate(key, co[:, None, :], si[:, None, :]).astype(BF16)
        scores = jnp.einsum("qkgd,skd->kgqs", query, key, preferred_element_type=F32) * SCALE
        masked = jnp.where(allowed[:rows, :rows], scores, -1e30)
        row_max = jnp.max(masked, axis=-1, keepdims=True)
        expo = jnp.exp(masked - row_max)
        prob = expo / jnp.sum(expo, axis=-1, keepdims=True)
        prob_low = prob.astype(BF16)
        mixed = jnp.einsum("kgqs,skd->qkgd", prob_low, value, preferred_element_type=F32)
        mixed = mixed.reshape(rows, HEADS * HEAD_DIM).astype(BF16)
        attn_out = dot(mixed, full_out)
        middle = picked + attn_out
        inv_two = rms(middle)
        normed_two = (middle * inv_two * gain_two).astype(BF16)
        gates, ups, hiddens = [], [], []
        ffn_out = None
        for block in range(nc // 2):
            gate_raw = dot(normed_two, gu_all[block, 0])
            up_raw = dot(normed_two, gu_all[block, 1])
            gates.append(gate_raw)
            ups.append(up_raw)
            hidden = (jax.nn.silu(gate_raw) * up_raw).astype(BF16)
            hiddens.append(hidden)
            part = dot_nt(hidden, dn_all[block])
            ffn_out = part if ffn_out is None else ffn_out + part
        both = attn_out + ffn_out
        updated = picked + gate_value[:, None] * both
        stream = jnp.concatenate([updated, stream[rows:]], axis=0)
        kept.append(
            (picked, gate_value, inv_one, normed, query, key, value, prob, prob_low, mixed,
             middle, inv_two, normed_two, gates, ups, hiddens, both)
        )

    output = dot_tn(chosen, stream.astype(BF16)).astype(BF16)

    router_grads, gain_one_grad, gain_two_grad = [None] * STEPS, 0.0, 0.0
    stacks = [[] for _ in range(8)]
    per_block = [[[] for _ in range(nc // 2)] for _ in range(3)]
    for step in reversed(range(STEPS)):
        rows = counts[step]
        (picked, gate_value, inv_one, normed, query, key, value, prob, prob_low, mixed,
         middle, inv_two, normed_two, gates, ups, hiddens, both) = kept[step]
        co, si = cosine[:rows], sine[:rows]
        grad_new = grad_stream[:rows]
        grad_logit = jnp.sum(grad_new * both, axis=1) * gate_value * (1.0 - gate_value)
        grad_branch = gate_value[:, None] * grad_new
        grad_ffn = grad_branch.astype(BF16)
        grad_n2 = None
        for block in range(nc // 2):
            grad_hidden = dot(grad_ffn, dn_all[block])
            gate_raw, up_raw = gates[block], ups[block]
            sig = jax.nn.sigmoid(gate_raw)
            act = gate_raw * sig
            grad_up = (grad_hidden * act).astype(BF16)
            grad_gate = (grad_hidden * up_raw * (sig + act * (1.0 - sig))).astype(BF16)
            part = dot_nt(grad_gate, gu_all[block, 0]) + dot_nt(grad_up, gu_all[block, 1])
            grad_n2 = part if grad_n2 is None else grad_n2 + part
            per_block[0][block].append(grad_gate)
            per_block[1][block].append(grad_up)
            per_block[2][block].append(hiddens[block])
        gain_two_grad = gain_two_grad + jnp.sum(grad_n2 * middle * inv_two, axis=0)
        grad_middle = rms_back(middle, inv_two, gain_two, grad_n2)
        grad_attn = (grad_branch + grad_middle).astype(BF16)
        grad_mixed = dot_nt(grad_attn, full_out).astype(BF16)
        grad_mixed = grad_mixed.reshape(rows, KV_HEADS, GROUPS, HEAD_DIM)
        grad_prob = jnp.einsum("qkgd,skd->kgqs", grad_mixed, value, preferred_element_type=F32)
        grad_value = jnp.einsum("kgqs,qkgd->skd", prob_low, grad_mixed, preferred_element_type=F32)
        grad_value = grad_value.reshape(rows, -1).astype(BF16)
        row_dot = jnp.sum(prob * grad_prob, axis=-1, keepdims=True)
        grad_scores = (prob * (grad_prob - row_dot)).astype(BF16)
        grad_query = jnp.einsum("kgqs,skd->qkgd", grad_scores, key, preferred_element_type=F32)
        grad_key = jnp.einsum("kgqs,qkgd->skd", grad_scores, query, preferred_element_type=F32)
        grad_query = rotate(grad_query * SCALE, co[:, None, None, :], -si[:, None, None, :])
        grad_key = rotate(grad_key * SCALE, co[:, None, :], -si[:, None, :])
        grad_query = grad_query.reshape(rows, -1).astype(BF16)
        grad_key = grad_key.reshape(rows, -1).astype(BF16)
        grad_n1 = dot_nt(grad_query, full_query) + dot_nt(grad_key, full_key)
        grad_n1 = grad_n1 + dot_nt(grad_value, full_value)
        gain_one_grad = gain_one_grad + jnp.sum(grad_n1 * picked * inv_one, axis=0)
        grad_norm = rms_back(picked, inv_one, gain_one, grad_n1)
        router_grads[step] = jnp.dot(grad_logit, picked, precision=highest)
        grad_picked = (
            grad_new + grad_middle + grad_norm + grad_logit[:, None] * router_cols[:, step][None, :]
        )
        grad_stream = jnp.concatenate([grad_picked, grad_stream[rows:]], axis=0)
        for where, item in zip(
            stacks,
            (normed, grad_query, grad_key, grad_value, mixed, grad_attn, normed_two, grad_ffn),
        ):
            where.append(item)
    token_grad = dot_tn(chosen, grad_stream.astype(BF16)).astype(BF16)

    normed, grad_query, grad_key, grad_value, mixed, grad_attn, normed_two, grad_ffn = [
        jnp.concatenate(items, axis=0) for items in stacks
    ]
    gu_grads, dn_grads = [], []
    for block in range(nc // 2):
        grad_gate, grad_up, hidden = [
            jnp.concatenate(per_block[i][block], axis=0) for i in range(3)
        ]
        gu_grads.append(dot_tn(normed_two, grad_gate).astype(BF16))
        gu_grads.append(dot_tn(normed_two, grad_up).astype(BF16))
        dn_grads.append(dot_tn(grad_ffn, hidden).astype(BF16))
    gu_grads = jnp.concatenate(gu_grads, axis=0)
    dn_grads = jnp.concatenate(dn_grads, axis=0)
    gu_part = lax.psum_scatter(gu_grads, ("col", "row"), scatter_dimension=0, tiled=True)
    dn_part = lax.psum_scatter(dn_grads, ("row", "col"), scatter_dimension=0, tiled=True)

    grads = [
        dot_tn(normed, grad_query), dot_tn(normed, grad_key), dot_tn(normed, grad_value),
        dot_tn(mixed, grad_attn),
    ]
    grads = [g.astype(BF16).reshape(width, nc, -1) for g in grads]
    grads = jnp.concatenate(grads, axis=2).reshape(nr, 2, att_rows, nc, -1)
    grads = grads.transpose(3, 0, 2, 1, 4).reshape(nc, nr, att_rows, -1)
    small = jnp.stack([gain_one_grad, *router_grads, gain_two_grad], axis=1).astype(BF16)
    small = small.reshape(nr, 5 * dr)
    extra = (att.shape[0] - att_rows) * att.shape[1]
    small = jnp.pad(small, ((0, 0), (0, extra - 5 * dr))).reshape(nr, -1, att.shape[1])
    small = jnp.broadcast_to(small[None], (nc, *small.shape))
    grads = jnp.concatenate([grads, small], axis=2).reshape(-1, att.shape[1])
    att_part = lax.psum_scatter(grads, ("col", "row"), scatter_dimension=0, tiled=True)

    mine = att_part[:att_rows]
    mine = unfold(mine).astype(F32)
    small = att_part[att_rows:].reshape(-1)[: 5 * dr].reshape(dr, 5).astype(F32)
    first, second = gu_part[:, :fc], gu_part[:, fc:]
    got = lax.ppermute(jnp.where(core == 0, second, first), "col", pairs)
    gate_block = jnp.where(core == 0, first, got).astype(F32)
    up_block = jnp.where(core == 0, got, second).astype(F32)
    down_block = dn_part.T.astype(F32)
    return (
        output[None],
        token_grad[None],
        small[:, 0],
        small[:, 1:4],
        mine[:, :qc],
        mine[:, qc : qc + kc],
        mine[:, qc + kc : qc + 2 * kc],
        mine[:, qc + 2 * kc :],
        small[:, 4],
        gate_block,
        up_block,
        down_block,
    )


def solution(mesh):
    seq = P(("row", "col"), None, None)
    ids = P(("row", "col"), None)
    mat = P("row", "col")
    return jax.shard_map(
        body,
        mesh=mesh,
        in_specs=(
            seq, ids, ids, ids, ids, P("row"), P("row", None), mat, mat, mat, mat, P("row"),
            mat, mat, mat, seq,
        ),
        out_specs=(
            seq, seq, P("row"), P("row", None), mat, mat, mat, mat, P("row"), mat, mat, mat,
        ),
        check_vma=False,
    )
```

time: 973 us -> 808 us (0.83)
  blocking collectives: 137 us -> 0 us
  waiting for transfers between devices: 406 us -> 378 us
  matrix products: 219 us -> 203 us
  other arithmetic: 44.7 us -> 59.4 us
    unnamed x24 -> x7, waiting for transfers between devices: 163 us -> 0.76 us
    all_gather x10 -> x0, blocking collectives: 112 us -> none  [the longest x1 19.1 us: body(): lax.all_gather(value_rows, 'col', axis=1, tiled=True)]
    all_gather x5 -> x3, waiting for transfers between devices: 41.4 us -> 118 us  [the longest x1 54.5 us: body(): att_all = lax.all_gather(att, ('col', 'row'), axis=0)]
    reduce_scatter x5 -> x2, waiting for transfers between devices: 202 us -> 258 us  [the longest x1 139 us: body(): lax.psum_scatter(gu_grads, ('col', 'row'), scatter_dimension=0, tiled=True)]
    concatenate x0 -> x10, local copies, waits for them, and re-layouts: none -> 41.2 us  [the longest x8 33.1 us: body(): grads = jnp.concatenate(grads, axis=2).reshape(nr, 2, att_rows, nc, -1)]
    gather x18 -> x0, local copies, waits for them, and re-layouts: 38.6 us -> none  [the longest x6 13.8 us: step_back(): grad_new = jnp.take(grad_stream, chosen, axis=0)]
    dot_general x87 -> x137, matrix products: 219 us -> 191 us  [the longest x50 61.6 us: dot(): return jnp.dot(a, b, preferred_element_type=F32)]
    concatenate x0 -> x7, other arithmetic: none -> 27.1 us  [the longest x1 15.5 us: body(): dn_grads = jnp.concatenate(dn_grads, axis=0)]
  transfers between devices with their start and end apart: 17 -> 8, of which waited for: 11 -> 6; matrix products, arithmetic and copies ran while one was open for 21% -> 28% of each run, Pallas kernels for 0% -> 0%
where the time goes in v1:
time: 808 us; the launch traced here: 796 us
  waiting for transfers between devices  378 us (47%)
  matrix products  203 us (25%)
  local copies, waits for them, and re-layouts  137 us (17%)
  other arithmetic  59.4 us (7%)
  between operations  18.3 us (2%)
    reduce_scatter x1, waiting for transfers between devices, body(): lax.psum_scatter(gu_grads, ('col', 'row'), scatter_dimension=0, tiled=True)  139 us
    reduce_scatter x1, waiting for transfers between devices, body(): lax.psum_scatter(grads, ('col', 'row'), scatter_dimension=0, tiled=True)  119 us
    dot_general x50, matrix products, dot(): return jnp.dot(a, b, preferred_element_type=F32)  61.6 us
    all_gather x1, waiting for transfers between devices, body(): att_all = lax.all_gather(att, ('col', 'row'), axis=0)  54.5 us
    all_gather x1, waiting for transfers between devices, body(): dn_all = lax.all_gather(dn, ('row', 'col'), axis=0)  48.8 us
    dot_general x18, matrix products, dot_tn(): lax.dot_general(a, b, (((0,), (0,)), ((), ())), preferred_element_type=F32)  48.4 us
    dot_general x48, matrix products, dot_nt(): lax.dot_general(a, b, (((1,), (1,)), ((), ())), preferred_element_type=F32)  45.9 us
    unnamed x596, local copies, waits for them, and re-layouts  34.7 us
  transfers between devices with their start and end apart: 8, of which 6 were waited for; matrix products, arithmetic and copies ran while one was open for 28% of the time, Pallas kernels for 0%

profile of v1, /device:TPU:0, one launch (start us, length us, event | category | flops | bytes accessed | tf_op | source)
XLA Modules:
  0.0 796.4 jit_solution(14755952502635066275)
XLA Ops:
  27.1 54.5 %all-gather.8.cloned.1.call-done = bf16[4096,640]{1,0:T(8,128)(2,1)} async-done(((bf16[128,640]{1,0:T(8,128)(2,1)}), bf16[4096,640]{1,0:T(8,128)(2,1)}) %all-gather.8.cloned.1.call-update) | async-done | bytes 5242896 | tf_op jit(solution)/shard_map/all_gather | solution.py:104
  81.6 5.1 slice.448
  88.9 7.8 copy.153
  96.7 10.2 %copy.154 = bf16[4,2,120,8,320]{2,1,0,4,3:T(2,128)(2,1)} copy(bf16[4,2,120,8,320]{2,4,1,0,3:T(8,128)(2,1)} %bitcast.612) | data formatting | bytes 9830400 | tf_op jit(solution)/shard_map/transpose | solution.py:115
  106.9 18.2 %reshape.617 = bf16[960,8,320]{0,2,1:T(8,128)(2,1)} reshape(bf16[4,2,120,8,320]{2,1,0,4,3:T(2,128)(2,1)} %copy.154) | data formatting | bytes 9830400 | tf_op jit(solution)/shard_map/reshape | solution.py:115
  135.6 7.3 fusion.354
  142.9 4.8 fusion.46
  147.7 2.3 multiply_reduce_fusion.5
  152.3 14.5 %all-gather.6.cloned.1.call-done = bf16[32,240,640]{2,1,0:T(8,128)(2,1)} async-done(((bf16[1,240,640]{2,1,0:T(8,128)(2,1)}), bf16[32,240,640]{2,1,0:T(8,128)(2,1)}) %all-gather.6.cloned.1.call-update) | async-done | bytes 9830416 | tf_op jit(solution)/shard_map/all_gather | solution.py:105
  166.8 2.5 fusion.216
  169.3 3.2 fusion.206
  172.6 2.5 fusion.186
  176.1 1.9 multiply_convert_fusion.14
  178.1 2.0 multiply_convert_fusion.15
  181.9 1.9 multiply_convert_fusion.16
  183.8 48.8 %all-gather.10.cloned.1.call-done = bf16[3840,640]{1,0:T(8,128)(2,1)} async-done(((bf16[120,640]{1,0:T(8,128)(2,1)}), bf16[3840,640]{1,0:T(8,128)(2,1)}) %all-gather.10.cloned.1.call-update) | async-done | bytes 4915216 | tf_op jit(solution)/shard_map/all_gather | solution.py:106
  232.6 2.5 fusion.235
  235.1 2.2 fusion.257
  238.7 2.6 fusion.346
  245.1 3.2 fusion.355
  248.5 2.7 convolution_convert_fusion.20
  272.1 2.3 convolution_convert_fusion.23
  274.5 2.4 multiply_reduce_fusion.20
  284.7 2.2 fusion.241
  300.0 1.9 multiply_reduce_fusion.17
  303.6 2.3 fusion.80
  328.8 2.6 fusion.10
  331.5 3.1 fusion.12
  344.1 2.8 convolution_convert_fusion.2
  346.9 2.4 convolution_convert_fusion.3
  349.4 2.5 convolution_convert_fusion.4
  351.8 2.4 convolution_convert_fusion.5
  363.1 2.0 fusion.197
  374.0 4.9 fusion.3
  378.9 15.5 %pad_maximum_fusion.2 = bf16[3840,640]{1,0:T(8,128)(2,1)} fusion(bf16[960,640]{1,0:T(8,128)(2,1)S(1)} %copy-done.69, bf16[960,640]{1,0:T(8,128)(2,1)S(1)} %copy-done.70, bf16[960,640]{1,0:T(8,128)(2,1)S(1)} %copy-done.71, bf16[960,640]{1,0:T(8,128)(2,1)S(1)} %copy-done.72), kind=kLoop, calls=%fused_computation.13 | loop fusion | flops 19660800 | bytes 9830400 | tf_op jit(solution)/shard_map/concatenate | solution.py:250
  394.7 10.1 %fusion.5 = bf16[5,3,384,384]{2,3,1,0:T(8,128)(2,1)} fusion(f32[5,384,384,3]{2,1,3,0:T(8,128)} %get-tuple-element.226, f32[5,3,384]{2,1,0:T(4,128)S(1)} %get-tuple-element.225, f32[5,3,384,384]{2,3,1,0:T(8,128)} %get-tuple-element.189, f32[5,3,384]{2,1,0:T(4,128)S(1)} %copy-done.192), kind=kLoop, calls=%fused_computation.7 | loop fusion | flops 8847360 | bytes 22164480 | tf_op jit(solution)/shard_map/convert_element_type | solution.py:215
  404.9 4.1 fusion.68
  416.4 2.2 multiply_reduce_fusion.1
  423.3 4.7 convolution_convert_fusion
  428.0 5.4 concatenate.222
  433.5 4.4 copy.174
  437.9 2.7 convolution_convert_fusion.17
  440.5 4.9 concatenate.219
  445.4 2.1 copy.173
  447.5 2.7 convolution_convert_fusion.18
  450.2 4.9 concatenate.217
  455.1 2.0 copy.172
  457.2 4.4 convolution_convert_fusion.1
  461.5 5.0 concatenate.215
  466.6 4.3 copy.171
  470.9 3.8 pad_maximum_fusion
  475.9 5.2 pad_maximum_fusion.1
  481.1 7.9 copy.177
  490.4 3.6 fusion.21
  494.1 2.4 fusion.22
  496.5 2.4 fusion.23
  499.0 2.5 fusion.24
  501.5 2.4 fusion.25
  504.0 2.4 fusion.26
  506.4 2.4 fusion.27
  508.8 2.4 fusion.28
  515.4 2.1 add_convert_fusion
  520.8 118.8 %reduce-scatter.6.cloned.1.call-done = bf16[128,640]{1,0:T(8,128)(2,1)} async-done(((bf16[4096,640]{1,0:T(8,128)(2,1)}), bf16[128,640]{1,0:T(8,128)(2,1)}) %reduce-scatter.6.cloned.1.call-update) | async-done | bytes 163856 | tf_op jit(solution)/shard_map/reduce_scatter | solution.py:267
  642.7 139.5 %reduce-scatter.8.cloned.1.call-done = bf16[240,640]{1,0:T(8,128)(2,1)} async-done(((bf16[7680,640]{1,0:T(8,128)(2,1)}), bf16[240,640]{1,0:T(8,128)(2,1)}) %reduce-scatter.8.cloned.1.call-update) | async-done | bytes 307216 | tf_op jit(solution)/shard_map/reduce_scatter | solution.py:251
  (849 shorter events, 166.3 us)
Async XLA Ops:
  7.2 14.8 %copy-start = (bf16[1,512,960]{1,2,0:T(8,128)(2,1)S(1)}, bf16[1,512,960]{1,2,0:T(8,128)(2,1)}, u32[]{:S(2)}) copy-start(bf16[1,512,960]{1,2,0:T(8,128)(2,1)} %param.31) | copy-start | bytes 2949124
  7.2 7.3 copy-start.184
  7.2 74.4 %all-gather.8.cloned.1.call-start = ((), (), s32[]{:S(2)}) async-start(), calls=%async_computation.6 | async-start | bytes 5406720 | tf_op jit(solution)/shard_map/all_gather | solution.py:104
  11.5 6.6 copy-start.238
  11.5 6.7 copy-start.236
  11.5 6.9 copy-start.237
  11.5 7.3 copy-start.201
  13.4 153.4 %all-gather.6.cloned.1.call-start = ((), (), s32[]{:S(2)}) async-start(), calls=%async_computation.3 | async-start | bytes 10137600 | tf_op jit(solution)/shard_map/all_gather | solution.py:105
  14.8 1.6 collective-permute-start
  17.3 215.3 %all-gather.10.cloned.1.call-start = ((), (), s32[]{:S(2)}) async-start(), calls=%async_computation.7 | async-start | bytes 5068800 | tf_op jit(solution)/shard_map/all_gather | solution.py:106
  18.1 501.1 %reduce-scatter.10.cloned.1.call-start = ((), (), s32[]{:S(2)}) async-start(), calls=%async_computation.8 | async-start | bytes 5068800
  18.8 4.9 copy-start.234
  21.9 111.4 %copy-start.64 = (f32[384,32]{0,1:T(8,128)}, f32[384,32]{0,1:T(8,128)S(1)}, u32[]{:S(2)}) copy-start(f32[384,32]{0,1:T(8,128)S(1)} %get-tuple-element.187) | copy-start | bytes 147460
  25.4 212.8 %copy-start.3 = (f32[512,960]{0,1:T(8,128)}, f32[512,960]{0,1:T(8,128)S(1)}, u32[]{:S(2)}) copy-start(f32[512,960]{0,1:T(8,128)S(1)} %fusion.86) | copy-start | bytes 5898244
  25.6 61.1 %copy-start.197 = (f32[384]{0:T(512)}, f32[384]{0:T(512)S(1)}, u32[]{:S(2)}) copy-start(f32[384]{0:T(512)S(1)} %multiply_reduce_fusion.6) | copy-start | bytes 4612
  25.6 103.9 %copy-start.189 = (f32[384]{0:T(512)}, f32[384]{0:T(512)S(1)}, u32[]{:S(2)}) copy-start(f32[384]{0:T(512)S(1)} %add_rsqrt_fusion.1) | copy-start | bytes 4612
  130.4 5.2 copy-start.87
  130.4 5.2 copy-start.89
  134.4 8.5 %copy-start.66 = (bf16[384,5,3,32]{0,3,2,1:T(8,128)(2,1)}, bf16[384,5,3,32]{0,3,2,1:T(8,128)(2,1)S(1)}, u32[]{:S(2)}) copy-start(bf16[384,5,3,32]{0,3,2,1:T(8,128)(2,1)S(1)} %get-tuple-element.127) | copy-start | bytes 1105924
  150.1 19.2 %copy-start.202 = (f32[384]{0:T(512)}, f32[384]{0:T(512)S(1)}, u32[]{:S(2)}) copy-start(f32[384]{0:T(512)S(1)} %get-tuple-element.107) | copy-start | bytes 4612
  166.8 8.2 %copy-start.2 = (bf16[32,240,640]{2,1,0:T(8,128)(2,1)S(1)}, bf16[32,240,640]{2,1,0:T(8,128)(2,1)}, u32[]{:S(2)}) copy-start(bf16[32,240,640]{2,1,0:T(8,128)(2,1)} %all-gather.6.cloned.1.call-done) | copy-start | bytes 29491204
  169.3 6.8 copy-start.259
  172.6 5.5 copy-start.257
  175.0 5.0 copy-start.253
  176.1 5.8 copy-start.255
  181.8 53.2 %copy-start.91 = (bf16[384,640]{1,0:T(8,128)(2,1)}, bf16[384,640]{1,0:T(8,128)(2,1)S(1)}, u32[]{:S(2)}) copy-start(bf16[384,640]{1,0:T(8,128)(2,1)S(1)} %get-tuple-element.193) | copy-start | bytes 1474564
  245.1 7.4 slice-start
  248.4 6.2 slice-start.2
  254.6 7.7 copy-start.114
  258.0 7.7 copy-start.209
  267.4 16.9 %copy-start.29 = (f32[256,960]{0,1:T(8,128)}, f32[256,960]{0,1:T(8,128)S(1)}, u32[]{:S(2)}) copy-start(f32[256,960]{0,1:T(8,128)S(1)} %get-tuple-element.104) | copy-start | bytes 2949124
  272.1 16.7 %slice-start.3 = ((s8[9830400]{0:T(1024)(128)(4,1)}), s8[1441792]{0:T(1024)(128)(4,1)S(1)}, s32[]{:S(2)}) async-start(s8[9830400]{0:T(1024)(128)(4,1)} %bitcast.548), calls=%async_computation.12 | async-start | bytes 2883584
  274.5 14.3 %slice-start.4 = ((s8[9830400]{0:T(1024)(128)(4,1)}), s8[4194304]{0:T(1024)(128)(4,1)S(1)}, s32[]{:S(2)}) async-start(s8[9830400]{0:T(1024)(128)(4,1)} %bitcast.548), calls=%async_computation.13 | async-start | bytes 8388608
  276.9 23.1 %copy-start.38 = (f32[128,960]{0,1:T(8,128)}, f32[128,960]{0,1:T(8,128)S(1)}, u32[]{:S(2)}) copy-start(f32[128,960]{0,1:T(8,128)S(1)} %get-tuple-element.100) | copy-start | bytes 1474564
  276.9 23.1 %copy-start.225 = (f32[128]{0:T(128)}, f32[128]{0:T(128)S(1)}, u32[]{:S(2)}) copy-start(f32[128]{0:T(128)S(1)} %add_rsqrt_fusion.4) | copy-start | bytes 1540
  277.1 17.3 %copy-start.44 = (bf16[128,960]{0,1:T(8,128)(2,1)}, bf16[128,960]{0,1:T(8,128)(2,1)S(1)}, u32[]{:S(2)}) copy-start(bf16[128,960]{0,1:T(8,128)(2,1)S(1)} %multiply_convert_fusion.31) | copy-start | bytes 737284
  282.4 6.4 slice-start.5
  282.4 9.8 %slice-start.11 = ((s8[4915200]{0:T(1024)(128)(4,1)}), s8[4194304]{0:T(1024)(128)(4,1)S(1)}, s32[]{:S(2)}) async-start(s8[4915200]{0:T(1024)(128)(4,1)} %bitcast.581), calls=%async_computation.20 | async-start | bytes 8388608
  284.6 15.3 %copy-start.215 = (f32[128]{0:T(128)}, f32[128]{0:T(128)S(1)}, u32[]{:S(2)}) copy-start(f32[128]{0:T(128)S(1)} %fusion.84) | copy-start | bytes 1540
  288.8 6.9 copy-start.157
  288.8 10.2 %copy-start.172 = (bf16[128,640]{1,0:T(8,128)(2,1)}, bf16[128,640]{1,0:T(8,128)(2,1)S(1)}, u32[]{:S(2)}) copy-start(bf16[128,640]{1,0:T(8,128)(2,1)S(1)} %get-tuple-element.154) | copy-start | bytes 491524
  291.6 6.9 copy-start.174
  293.4 6.1 copy-start.178
  295.0 5.0 copy-start.180
  308.3 5.3 slice-start.13
  309.2 6.2 slice-start.6
  315.4 7.6 copy-start.134
  317.9 5.7 copy-start.138
  341.5 29.3 %copy-start.32 = (f32[256,960]{0,1:T(8,128)}, f32[256,960]{0,1:T(8,128)S(1)}, u32[]{:S(2)}) copy-start(f32[256,960]{0,1:T(8,128)S(1)} %multiply_add_fusion.1) | copy-start | bytes 2949124
  368.9 5.1 slice-start.18
  368.9 5.1 slice-start.19
  374.0 4.9 copy-start.69
  374.0 4.9 copy-start.70
  374.0 4.9 copy-start.71
  394.4 245.2 %reduce-scatter.6.cloned.1.call-start = ((), (), s32[]{:S(2)}) async-start(), calls=%async_computation.4 | async-start | bytes 5406720 | tf_op jit(solution)/shard_map/reduce_scatter | solution.py:267
  394.7 10.1 %copy-start.67 = (bf16[384,5,3,32]{0,3,2,1:T(8,128)(2,1)S(1)}, bf16[384,5,3,32]{0,3,2,1:T(8,128)(2,1)}, u32[]{:S(2)}) copy-start(bf16[384,5,3,32]{0,3,2,1:T(8,128)(2,1)} %copy-done.66) | copy-start | bytes 1105924
  394.7 10.1 %copy-start.68 = (bf16[384,5,3,32]{0,3,2,1:T(8,128)(2,1)S(1)}, bf16[384,5,3,32]{0,3,2,1:T(8,128)(2,1)}, u32[]{:S(2)}) copy-start(bf16[384,5,3,32]{0,3,2,1:T(8,128)(2,1)} %get-tuple-element.128) | copy-start | bytes 1105924
  440.5 7.0 copy-start.86
  440.5 7.0 copy-start.133
  450.2 7.0 copy-start.62
  450.2 7.0 copy-start.75
  489.0 293.2 %reduce-scatter.8.cloned.1.call-start = ((), (), s32[]{:S(2)}) async-start(), calls=%async_computation.5 | async-start | bytes 10137600 | tf_op jit(solution)/shard_map/reduce_scatter | solution.py:251
  782.2 7.2 copy-start.1
  783.4 3.1 collective-permute-start.1
  (237 other events, 588.4 us)
Sparse Core Ops, SparseCore 0:
  13.5 68.0 all-gather.7
  85.0 81.7 all-gather.5
  169.7 62.8 all-gather.9
  394.5 99.2 reduce-scatter.9
  495.9 143.6 reduce-scatter.5
  645.5 136.6 reduce-scatter.7

commit v2 on v1

--- a/solution.py
+++ b/solution.py
@@ -1,7 +1,10 @@
 import jax
 import jax.numpy as jnp
 from jax import lax
+from jax.experimental import pallas as pl
+from jax.experimental.pallas import tpu as pltpu
 from jax.sharding import PartitionSpec as P
+
 
 HEADS = 15
 KV_HEADS = 5
@@ -79,6 +82,192 @@
     return jnp.concatenate([block[:, :half], block[:, half:]], axis=0)
 
 
+def to_x(value):
+    return lax.ppermute(value, "row", [(i, i ^ 1) for i in range(4)])
+
+
+def to_y(value):
+    return lax.ppermute(value, "row", [(i, i ^ 2) for i in range(4)])
+
+
+def to_core(value):
+    return lax.ppermute(value, "col", [(i, i ^ 1) for i in range(8)])
+
+
+def to_up(value, low, high):
+    return lax.ppermute(value, "col", [(i, i + 2) for i in range(2 * low, 2 * high + 2)])
+
+
+def to_down(value, low, high):
+    return lax.ppermute(value, "col", [(i, i - 2) for i in range(2 * low, 2 * high + 2)])
+
+
+def add_low(*values):
+    total = values[0].astype(F32)
+    for value in values[1:]:
+        total = total + value.astype(F32)
+    return total.astype(BF16)
+
+
+def place_kernel(cuts, first, where, *refs):
+    sources = refs[:10]
+    outs = refs[10 if first else 13 :][:3]
+    bufs, sem_in, sem_out = refs[-5:-2], refs[-2], refs[-1]
+    plane, row, core = where[0], where[1], where[2]
+    arrivals, leaves = [], []
+    for side in range(2):
+        p, a, b, dx, dy = sources[side * 5 : side * 5 + 5]
+        for rel in range(4):
+            slot = side * 4 + rel
+            for part in range(3):
+                low, high = cuts[part], cuts[part + 1]
+                if rel < 3:
+                    src = (p, a, b)[rel].at[pl.ds(low, high - low)]
+                elif part < 2:
+                    src = dx.at[pl.ds(low, high - low)]
+                else:
+                    src = dy
+                k = slot * 3 + part
+                arrivals.append(pltpu.make_async_copy(src, bufs[part].at[slot], sem_in.at[k]))
+                r = jnp.bitwise_xor(row, rel)
+                c = jnp.bitwise_xor(core, side)
+                dst = outs[part].at[r, plane, c] if part == 1 else outs[part].at[plane, c, r]
+                leaves.append(pltpu.make_async_copy(bufs[part].at[slot], dst, sem_out.at[k]))
+    for copy in arrivals:
+        copy.start()
+    for arrive, leave in zip(arrivals, leaves):
+        arrive.wait()
+        leave.start()
+    for copy in leaves:
+        copy.wait()
+
+
+def place(cuts, where, sources, held):
+    width = sources[0].shape[1]
+    sizes = [high - low for low, high in zip(cuts, cuts[1:])]
+    shapes = [(4, 2, 4, sizes[0], width), (4, 4, 2, sizes[1], width), (4, 2, 4, sizes[2], width)]
+    first = held is None
+    anywhere = pl.BlockSpec(memory_space=pl.ANY)
+    inputs = list(sources) + ([] if first else list(held))
+    return pl.pallas_call(
+        lambda *refs: place_kernel(cuts, first, *refs),
+        grid_spec=pltpu.PrefetchScalarGridSpec(
+            num_scalar_prefetch=1,
+            grid=(1,),
+            in_specs=[anywhere] * len(inputs),
+            out_specs=[anywhere] * 3,
+            scratch_shapes=[pltpu.VMEM((8, n, width), BF16) for n in sizes]
+            + [pltpu.SemaphoreType.DMA((24,)), pltpu.SemaphoreType.DMA((24,))],
+        ),
+        out_shape=[jax.ShapeDtypeStruct(shape, BF16) for shape in shapes],
+        input_output_aliases={} if first else {11: 0, 12: 1, 13: 2},
+        compiler_params=pltpu.CompilerParams(vmem_limit_bytes=24 << 20),
+        cost_estimate=pl.CostEstimate(flops=0, bytes_accessed=10 << 20, transcendentals=0),
+        name="place",
+    )(where, *inputs)
+
+
+def gather_units(unit, cuts):
+    half = cuts[2]
+    z, core = lax.axis_index("col") // 2, lax.axis_index("col") % 2
+    row = lax.axis_index("row")
+    u, d = [unit], [unit]
+    for hop in range(3):
+        u.append(to_up(u[-1], hop, 2))
+        d.append(to_down(d[-1], 1, 3 - hop))
+    p1 = jnp.where((z == 3) | (z == 1), u[1], d[1])
+    u1, d1, _ = lax.optimization_barrier((u[1], d[1], p1))
+    p2 = jnp.where(z == 0, d[2], jnp.where(z == 1, d1, jnp.where(z == 2, u1, u[2])))
+    u2, d2, _ = lax.optimization_barrier((u[2], d[2], p2))
+    p3 = jnp.where(z == 0, d[3], jnp.where(z == 1, d2, jnp.where(z == 2, u2, u[3])))
+    order = jnp.array([[0, 1, 2, 3], [1, 0, 2, 3], [2, 3, 1, 0], [3, 2, 1, 0]], jnp.int32)[z]
+    held = None
+    for i, p in enumerate((unit, p1, p2, p3)):
+        a, b = to_x(p), to_y(p)
+        dx, dy = to_x(b[:half]), to_y(a[half:])
+        if i == 0:
+            dx, dy, _, _ = lax.optimization_barrier((dx, dy, u[3], d[3]))
+        if i == 1:
+            dx, dy, _ = lax.optimization_barrier((dx, dy, p3))
+        mine = (p, a, b, dx, dy)
+        other = [to_core(v) for v in mine]
+        where = jnp.stack([order[i], row, core]).astype(jnp.int32)
+        held = place(cuts, where, [*mine, *other], held)
+    return held
+
+
+def pick_kernel(cuts, where, *refs):
+    sources, outs = refs[:3], refs[3:5]
+    bufs, sem_in, sem_out = refs[-5:-2], refs[-2], refs[-1]
+    plane, row, core = where[0], where[1], where[2]
+    arrivals, leaves = [], []
+    for side in (1, 0):
+        for rel in range(4):
+            slot = side * 4 + rel
+            r = jnp.bitwise_xor(row, rel)
+            c = jnp.bitwise_xor(core, side)
+            for part in range(3):
+                low, high = cuts[part], cuts[part + 1]
+                k = slot * 3 + part
+                src = sources[part]
+                src = src.at[r, plane, c] if part == 1 else src.at[plane, c, r]
+                arrivals.append(pltpu.make_async_copy(src, bufs[part].at[slot], sem_in.at[k]))
+                dst = outs[side].at[rel, pl.ds(low, high - low)]
+                leaves.append(pltpu.make_async_copy(bufs[part].at[slot], dst, sem_out.at[k]))
+    for copy in arrivals:
+        copy.start()
+    for arrive, leave in zip(arrivals, leaves):
+        arrive.wait()
+        leave.start()
+    for copy in leaves:
+        copy.wait()
+
+
+def pick(cuts, where, sources):
+    width = sources[0].shape[-1]
+    sizes = [high - low for low, high in zip(cuts, cuts[1:])]
+    anywhere = pl.BlockSpec(memory_space=pl.ANY)
+    return pl.pallas_call(
+        lambda *refs: pick_kernel(cuts, *refs),
+        grid_spec=pltpu.PrefetchScalarGridSpec(
+            num_scalar_prefetch=1,
+            grid=(1,),
+            in_specs=[anywhere] * 3,
+            out_specs=[anywhere] * 2,
+            scratch_shapes=[pltpu.VMEM((8, n, width), BF16) for n in sizes]
+            + [pltpu.SemaphoreType.DMA((24,)), pltpu.SemaphoreType.DMA((24,))],
+        ),
+        out_shape=[jax.ShapeDtypeStruct((4, cuts[3], width), BF16)] * 2,
+        compiler_params=pltpu.CompilerParams(vmem_limit_bytes=24 << 20),
+        cost_estimate=pl.CostEstimate(flops=0, bytes_accessed=10 << 20, transcendentals=0),
+        name="pick",
+    )(where, *sources)
+
+
+def reduce_units(parts, cuts):
+    half = cuts[2]
+    z, core = lax.axis_index("col") // 2, lax.axis_index("col") % 2
+    row = lax.axis_index("row")
+    order = jnp.array([[3, 2, 1, 0], [3, 2, 0, 1], [0, 1, 3, 2], [0, 1, 2, 3]], jnp.int32)[z]
+    sums = []
+    for i in range(4):
+        where = jnp.stack([order[i], row, core]).astype(jnp.int32)
+        mine, other = pick(cuts, where, parts)
+        g = add_low(mine, to_core(other))
+        dx, dy = to_x(g[3][:half]), to_y(g[3][half:])
+        for_x = jnp.concatenate([g[1][:half], add_low(g[1][half:], dy)], axis=0)
+        for_y = jnp.concatenate([add_low(g[2][:half], dx), g[2][half:]], axis=0)
+        ax, ay = to_x(for_x), to_y(for_y)
+        sums.append(add_low(g[0], ax, ay))
+    one, two, three, own = sums
+    u, d = to_up(one, 0, 0), to_down(one, 3, 3)
+    u = to_up(add_low(jnp.where(z == 0, two, one), u), 0, 1)
+    d = to_down(add_low(jnp.where(z == 3, two, one), d), 2, 3)
+    u = to_up(add_low(jnp.where(z == 1, two, three), u), 0, 2)
+    d = to_down(add_low(jnp.where(z == 2, two, three), d), 1, 3)
+    return own.astype(F32) + u.astype(F32) + d.astype(F32)
+
+
 def body(
     tokens, segment_ids, route_one, route_two, route_three, attn_gain, router,
     w_query, w_key, w_value, w_out, ffn_gain, w_gate, w_up, w_down, cotangent,
@@ -101,9 +290,14 @@
         jnp.concatenate([swapped, w_up], axis=1),
     )
     dn = w_down.T
-    att_all = lax.all_gather(att, ("col", "row"), axis=0)
-    gu_all = lax.all_gather(gu, ("col", "row"), axis=0)
-    dn_all = lax.all_gather(dn, ("row", "col"), axis=0)
+    cuts = (0, att.shape[0], att.shape[0] + dn.shape[0], att.shape[0] + dn.shape[0] + gu.shape[0])
+    direct = (nr, nc) == (4, 8)
+    if direct:
+        att_all, dn_all, gu_all = gather_units(jnp.concatenate([att, dn, gu], axis=0), cuts)
+    else:
+        att_all = lax.all_gather(att, ("col", "row"), axis=0)
+        gu_all = lax.all_gather(gu, ("col", "row"), axis=0)
+        dn_all = lax.all_gather(dn, ("row", "col"), axis=0)
     fw = 2 * fc
     gu_all = gu_all.reshape(nc // 2, 2, width, fw)
     dn_all = dn_all.reshape(nr, width, w_down.shape[0])
@@ -248,9 +442,6 @@
         dn_grads.append(dot_tn(grad_ffn, hidden).astype(BF16))
     gu_grads = jnp.concatenate(gu_grads, axis=0)
     dn_grads = jnp.concatenate(dn_grads, axis=0)
-    gu_part = lax.psum_scatter(gu_grads, ("col", "row"), scatter_dimension=0, tiled=True)
-    dn_part = lax.psum_scatter(dn_grads, ("row", "col"), scatter_dimension=0, tiled=True)
-
     grads = [
         dot_tn(normed, grad_query), dot_tn(normed, grad_key), dot_tn(normed, grad_value),
         dot_tn(mixed, grad_attn),
@@ -264,15 +455,27 @@
     small = jnp.pad(small, ((0, 0), (0, extra - 5 * dr))).reshape(nr, -1, att.shape[1])
     small = jnp.broadcast_to(small[None], (nc, *small.shape))
     grads = jnp.concatenate([grads, small], axis=2).reshape(-1, att.shape[1])
-    att_part = lax.psum_scatter(grads, ("col", "row"), scatter_dimension=0, tiled=True)
+    if direct:
+        parts = (
+            grads.reshape(4, 2, 4, -1, fw),
+            dn_grads.reshape(4, 4, 2, -1, fw),
+            gu_grads.reshape(4, 2, 4, -1, fw),
+        )
+        total = reduce_units(parts, cuts)
+        att_part, dn_part, gu_part = [total[a:b] for a, b in zip(cuts, cuts[1:])]
+    else:
+        att_part = lax.psum_scatter(grads, ("col", "row"), scatter_dimension=0, tiled=True)
+        gu_part = lax.psum_scatter(gu_grads, ("col", "row"), scatter_dimension=0, tiled=True)
+        dn_part = lax.psum_scatter(dn_grads, ("row", "col"), scatter_dimension=0, tiled=True)
 
     mine = att_part[:att_rows]
     mine = unfold(mine).astype(F32)
     small = att_part[att_rows:].reshape(-1)[: 5 * dr].reshape(dr, 5).astype(F32)
     first, second = gu_part[:, :fc], gu_part[:, fc:]
-    got = lax.ppermute(jnp.where(core == 0, second, first), "col", pairs)
-    gate_block = jnp.where(core == 0, first, got).astype(F32)
-    up_block = jnp.where(core == 0, got, second).astype(F32)
+    got = lax.ppermute(jnp.where(core == 0, second, first).astype(BF16), "col", pairs)
+    first, second, got = first.astype(F32), second.astype(F32), got.astype(F32)
+    gate_block = jnp.where(core == 0, first, got)
+    up_block = jnp.where(core == 0, got, second)
     down_block = dn_part.T.astype(F32)
     return (
         output[None],

time: 808 us -> 648 us (0.80)
  waiting for transfers between devices: 378 us -> 96 us
  starting transfers between devices: 1.26 us -> 79.7 us
  Pallas kernels: 0 us -> 67.9 us
  between operations: 18.3 us -> 5.9 us
  matrix products: 203 us -> 191 us
    reduce_scatter x2 -> x0, waiting for transfers between devices: 258 us -> none  [the longest x1 139 us: body(): lax.psum_scatter(gu_grads, ('col', 'row'), scatter_dimension=0, tiled=True)]
    all_gather x3 -> x0, waiting for transfers between devices: 118 us -> none  [the longest x1 54.5 us: body(): att_all = lax.all_gather(att, ('col', 'row'), axis=0)]
    ppermute x1 -> x69, waiting for transfers between devices: 0.01 us -> 96 us  [the longest x16 65.6 us: to_x(): return lax.ppermute(value, 'row', [(i, i ^ 1) for i in range(4)])]
    ppermute x1 -> x69, starting transfers between devices: 0.07 us -> 79.1 us  [the longest x6 26.4 us: to_up(): lax.ppermute(value, 'col', [(i, i + 2) for i in range(2 * low, 2 * high +...]
    pallas_call x0 -> x8, Pallas kernels: none -> 67.9 us  [the longest x4 34.2 us: place(): pl.pallas_call(lambda *refs: place_kernel(cuts, first, *refs), grid_spec=...]
    unnamed x596 -> x653, local copies, waits for them, and re-layouts: 34.7 us -> 51.9 us
    slice x2 -> x1, local copies, waits for them, and re-layouts: 12.9 us -> 2.74 us  [body(): aw = att_all[:, :, :att_rows].reshape(nc, nr, att_rows, 2, qc * 2 + kc * 2)]
    concatenate x1, other arithmetic: 15.5 us -> 5.85 us  [body(): dn_grads = jnp.concatenate(dn_grads, axis=0)]
  transfers between devices with their start and end apart: 8 -> 70, of which waited for: 6 -> 19; matrix products, arithmetic and copies ran while one was open for 28% -> 8% of each run, Pallas kernels for 0% -> 8%
where the time goes in v2:
time: 648 us; the launch traced here: 638 us
  matrix products  191 us (29%)
  local copies, waits for them, and re-layouts  134 us (21%)
  waiting for transfers between devices  96 us (15%)
  starting transfers between devices  79.7 us (12%)
  Pallas kernels  67.9 us (10%)
  other arithmetic  64.3 us (10%)
    ppermute x16, waiting for transfers between devices, to_x(): return lax.ppermute(value, 'row', [(i, i ^ 1) for i in range(4)])  65.6 us
    dot_general x50, matrix products, dot(): return jnp.dot(a, b, preferred_element_type=F32)  57.4 us
    unnamed x653, local copies, waits for them, and re-layouts  51.9 us
    dot_general x18, matrix products, dot_tn(): lax.dot_general(a, b, (((0,), (0,)), ((), ())), preferred_element_type=F32)  42.8 us
    dot_general x48, matrix products, dot_nt(): lax.dot_general(a, b, (((1,), (1,)), ((), ())), preferred_element_type=F32)  42.7 us
    pallas_call x4, Pallas kernels, place(): pl.pallas_call(lambda *refs: place_kernel(cuts, first, *refs), grid_spec=...  34.2 us
    pallas_call x4, Pallas kernels, pick(): pl.pallas_call(lambda *refs: pick_kernel(cuts, *refs), grid_spec=pltpu.Pr...  33.7 us
    concatenate x8, local copies, waits for them, and re-layouts, body(): grads = jnp.concatenate(grads, axis=2).reshape(nr, 2, att_rows, nc, -1)  28.4 us
  transfers between devices with their start and end apart: 70, of which 19 were waited for; matrix products, arithmetic and copies ran while one was open for 8% of the time, Pallas kernels for 8%

profile of v2, /device:TPU:0, one launch (start us, length us, event | category | flops | bytes accessed | tf_op | source)
XLA Modules:
  0.0 638.2 jit_solution(11337218993707306565)
XLA Ops:
  9.9 2.6 collective-permute-start.34
  12.8 5.4 collective-permute-start.4
  20.0 7.2 %collective-permute-done.34.refs_2_ = bf16[488,640]{1,0:T(8,128)(2,1)S(1)} collective-permute-done((bf16[488,640]{1,0:T(8,128)(2,1)S(1)}, bf16[488,640]{1,0:T(8,128)(2,1)S(1)}, u32[]{:S(2)}, u32[]{:S(2)}) %collective-permute-start.34) | collective-permute-done | bytes 624672 | tf_op jit(solution)/shard_map/ppermute | solution.py:86
  32.4 2.7 collective-permute-done.35.refs_3_
  42.9 3.2 fusion.93
  50.3 6.5 %collective-permute-done.25.refs_2_ = bf16[488,640]{1,0:T(8,128)(2,1)S(1)} collective-permute-done((bf16[488,640]{1,0:T(8,128)(2,1)S(1)}, bf16[488,640]{1,0:T(8,128)(2,1)S(1)}, u32[]{:S(2)}, u32[]{:S(2)}) %collective-permute-start.25) | collective-permute-done | bytes 624672 | tf_op jit(solution)/shard_map/ppermute | solution.py:86
  64.2 2.6 collective-permute-done.28.refs_5_
  68.9 7.7 %collective-permute-done.27.refs_4_ = bf16[248,640]{1,0:T(8,128)(2,1)S(1)} collective-permute-done((bf16[248,640]{1,0:T(8,128)(2,1)S(1)}, bf16[248,640]{1,0:T(8,128)(2,1)S(1)}, u32[]{:S(2)}, u32[]{:S(2)}) %collective-permute-start.27) | collective-permute-done | bytes 317472 | tf_op jit(solution)/shard_map/ppermute | solution.py:86
  83.0 4.4 collective-permute-done.19.refs_5_
  93.2 9.4 %collective-permute-done.18.refs_4_ = bf16[248,640]{1,0:T(8,128)(2,1)S(1)} collective-permute-done((bf16[248,640]{1,0:T(8,128)(2,1)S(1)}, bf16[248,640]{1,0:T(8,128)(2,1)S(1)}, u32[]{:S(2)}, u32[]{:S(2)}) %collective-permute-start.18) | collective-permute-done | bytes 317472 | tf_op jit(solution)/shard_map/ppermute | solution.py:86
  111.2 5.7 collective-permute-done.10.refs_5_
  118.8 8.1 %place.4 = (bf16[4,2,4,128,640]{4,3,2,1,0:T(8,128)(2,1)S(1)}, bf16[4,4,2,120,640]{4,3,2,1,0:T(8,128)(2,1)S(1)}, bf16[4,2,4,240,640]{4,3,2,1,0:T(8,128)(2,1)S(1)}) custom-call(s32[3]{0:T(128)S(1)} %add_add_fusion.7.refs_0_, bf16[488,640]{1,0:T(8,128)(2,1)S(1)} %pad_maximum_fusion.9.refs_1_, bf16[488,640]{1,0:T(8,128)(2,1)S(1)} %copy-done.7, ...), custom_call_target="tpu_custom_call" | custom-call | bytes 10485760 | tf_op jit(solution)/shard_map/place/pallas_call | solution.py:152
  126.9 8.4 %place.5 = (bf16[4,2,4,128,640]{4,3,2,1,0:T(8,128)(2,1)S(1)}, bf16[4,4,2,120,640]{4,3,2,1,0:T(8,128)(2,1)S(1)}, bf16[4,2,4,240,640]{4,3,2,1,0:T(8,128)(2,1)S(1)}) custom-call(s32[3]{0:T(128)S(1)} %add_add_fusion.6.refs_0_, bf16[488,640]{1,0:T(8,128)(2,1)S(1)} %broadcast_select_fusion.refs_1_, ...), custom_call_target="tpu_custom_call", output_to_operand_aliasing={{0}: (11, {}), {1}: (12, {}), {2}: (13, {})} | custom-call | bytes 10485760 | tf_op jit(solution)/shard_map/place/pallas_call | solution.py:152
  135.3 8.9 %place.6 = (bf16[4,2,4,128,640]{4,3,2,1,0:T(8,128)(2,1)S(1)}, bf16[4,4,2,120,640]{4,3,2,1,0:T(8,128)(2,1)S(1)}, bf16[4,2,4,240,640]{4,3,2,1,0:T(8,128)(2,1)S(1)}) custom-call(s32[3]{0:T(128)S(1)} %add_add_fusion.5.refs_0_, bf16[488,640]{1,0:T(8,128)(2,1)S(1)} %select_select_fusion.1.refs_1_, ...), custom_call_target="tpu_custom_call", output_to_operand_aliasing={{0}: (11, {}), {1}: (12, {}), {2}: (13, {})} | custom-call | bytes 10485760 | tf_op jit(solution)/shard_map/place/pallas_call | solution.py:152
  144.2 8.9 %place.7 = (bf16[4,2,4,128,640]{4,3,2,1,0:T(8,128)(2,1)S(1)}, bf16[4,4,2,120,640]{4,3,2,1,0:T(8,128)(2,1)S(1)}, bf16[4,2,4,240,640]{4,3,2,1,0:T(8,128)(2,1)S(1)}) custom-call(s32[3]{0:T(128)S(1)} %add_add_fusion.4.refs_0_, bf16[488,640]{1,0:T(8,128)(2,1)S(1)} %select_select_fusion.refs_1_, ...), custom_call_target="tpu_custom_call", output_to_operand_aliasing={{0}: (11, {}), {1}: (12, {}), {2}: (13, {})} | custom-call | bytes 10485760 | tf_op jit(solution)/shard_map/place/pallas_call | solution.py:152
  153.0 3.8 copy-done.2
  159.1 2.7 slice.790
  161.8 7.7 %copy.157 = bf16[8,4,120,640]{2,3,1,0:T(8,128)(2,1)} copy(bf16[8,4,120,640]{3,2,1,0:T(8,128)(2,1)} %slice.790) | data formatting | bytes 9830400
  169.6 10.2 %copy.106 = bf16[4,2,120,8,320]{2,1,0,4,3:T(2,128)(2,1)} copy(bf16[4,2,120,8,320]{2,4,1,0,3:T(8,128)(2,1)} %bitcast.777) | data formatting | bytes 9830400 | tf_op jit(solution)/shard_map/transpose | solution.py:309
  179.8 10.3 %reshape.622 = bf16[960,8,320]{0,2,1:T(8,128)(2,1)} reshape(bf16[4,2,120,8,320]{2,1,0,4,3:T(2,128)(2,1)} %copy.106) | data formatting | bytes 9830400 | tf_op jit(solution)/shard_map/reshape | solution.py:309
  190.0 3.9 fusion.328
  194.0 3.0 fusion.327
  202.7 6.3 fusion.334
  209.1 4.7 fusion.46
  232.4 2.6 fusion.325
  238.7 4.4 fusion.335
  243.2 2.8 convolution_convert_fusion.20
  325.6 2.7 fusion.10
  328.3 3.1 fusion.12
  354.6 3.0 multiply_reduce_fusion
  362.9 4.9 fusion.3
  367.8 9.8 %fusion.5 = bf16[5,3,384,384]{2,3,1,0:T(8,128)(2,1)} fusion(f32[5,384,384,3]{2,1,3,0:T(8,128)} %get-tuple-element.290, f32[5,3,384]{2,1,0:T(4,128)S(1)} %get-tuple-element.289, f32[5,3,384,384]{2,3,1,0:T(8,128)} %get-tuple-element.253, f32[5,3,384]{2,1,0:T(4,128)S(1)} %copy-done.237), kind=kLoop, calls=%fused_computation.7 | loop fusion | flops 8847360 | bytes 22164480 | tf_op jit(solution)/shard_map/convert_element_type | solution.py:409
  377.6 3.3 multiply_bitcast_fusion
  383.5 3.0 convolution_convert_fusion
  392.4 3.0 convolution_convert_fusion.1
  395.5 2.6 convolution_convert_fusion.10
  402.9 2.4 convolution_convert_fusion.13
  414.7 5.0 concatenate.226
  419.7 4.3 copy.122
  426.8 4.9 concatenate.221
  433.7 5.2 concatenate.219
  438.9 4.2 copy.119
  443.2 5.7 pad_maximum_fusion
  448.8 7.8 %copy.124 = bf16[4,2,4,120,640]{4,3,2,1,0:T(8,128)(2,1)} copy(bf16[4,2,4,120,640]{3,4,2,1,0:T(8,128)(2,1)} %bitcast.776) | data formatting | bytes 9830400 | tf_op jit(solution)/shard_map/concatenate | solution.py:457
  456.7 4.0 fusion.22
  460.7 2.4 fusion.23
  475.2 3.4 pad_maximum_fusion.1.refs_1_
  478.7 5.8 pad_maximum_fusion.2
  484.5 2.5 copy-done.3
  489.4 6.9 %pick.7 = (bf16[4,488,640]{2,1,0:T(8,128)(2,1)S(1)}, bf16[4,488,640]{2,1,0:T(8,128)(2,1)}) custom-call(s32[3]{0:T(128)S(1)} %get-tuple-element.295.refs_0_, bf16[4,2,4,128,640]{4,3,2,1,0:T(8,128)(2,1)S(1)} %copy-done.3, bf16[4,4,2,120,640]{4,3,2,1,0:T(8,128)(2,1)S(1)} %bitcast.720, bf16[4,2,4,240,640]{4,3,2,1,0:T(8,128)(2,1)S(1)} %bitcast.716), custom_call_target="tpu_custom_call" | custom-call | bytes 10485760 | tf_op jit(solution)/shard_map/pick/pallas_call | solution.py:230
  497.7 8.8 %pick.5 = (bf16[4,488,640]{2,1,0:T(8,128)(2,1)S(1)}, bf16[4,488,640]{2,1,0:T(8,128)(2,1)S(1)}) custom-call(s32[3]{0:T(128)S(1)} %get-tuple-element.293.refs_0_, bf16[4,2,4,128,640]{4,3,2,1,0:T(8,128)(2,1)S(1)} %copy-done.3, bf16[4,4,2,120,640]{4,3,2,1,0:T(8,128)(2,1)S(1)} %bitcast.721, bf16[4,2,4,240,640]{4,3,2,1,0:T(8,128)(2,1)S(1)} %bitcast.717), custom_call_target="tpu_custom_call" | custom-call | bytes 10485760 | tf_op jit(solution)/shard_map/pick/pallas_call | solution.py:230
  507.1 9.2 %pick.6 = (bf16[4,488,640]{2,1,0:T(8,128)(2,1)S(1)}, bf16[4,488,640]{2,1,0:T(8,128)(2,1)S(1)}) custom-call(s32[3]{0:T(128)S(1)} %get-tuple-element.294.refs_0_, bf16[4,2,4,128,640]{4,3,2,1,0:T(8,128)(2,1)S(1)} %copy-done.3, bf16[4,4,2,120,640]{4,3,2,1,0:T(8,128)(2,1)S(1)} %bitcast.722, bf16[4,2,4,240,640]{4,3,2,1,0:T(8,128)(2,1)S(1)} %bitcast.718), custom_call_target="tpu_custom_call" | custom-call | bytes 10485760 | tf_op jit(solution)/shard_map/pick/pallas_call | solution.py:230
  517.2 8.8 %pick.4 = (bf16[4,488,640]{2,1,0:T(8,128)(2,1)S(1)}, bf16[4,488,640]{2,1,0:T(8,128)(2,1)S(1)}) custom-call(s32[3]{0:T(128)S(1)} %get-tuple-element.292.refs_0_, bf16[4,2,4,128,640]{4,3,2,1,0:T(8,128)(2,1)S(1)} %copy-done.3, bf16[4,4,2,120,640]{4,3,2,1,0:T(8,128)(2,1)S(1)} %bitcast.723, bf16[4,2,4,240,640]{4,3,2,1,0:T(8,128)(2,1)S(1)} %bitcast.719), custom_call_target="tpu_custom_call" | custom-call | bytes 10485760 | tf_op jit(solution)/shard_map/pick/pallas_call | solution.py:230
  526.7 2.4 add_convert_fusion
  536.1 2.4 add_convert_fusion.1
  543.8 2.7 collective-permute-done.49
  550.3 16.4 %collective-permute-done.60 = bf16[488,640]{1,0:T(8,128)(2,1)S(1)} collective-permute-done((bf16[488,640]{1,0:T(8,128)(2,1)S(1)}, bf16[488,640]{1,0:T(8,128)(2,1)S(1)}, u32[]{:S(2)}, u32[]{:S(2)}) %collective-permute-start.60) | collective-permute-done | bytes 624672 | tf_op jit(solution)/shard_map/ppermute | solution.py:86
  569.1 4.9 collective-permute-start.63
  575.0 11.3 %collective-permute-done.50 = bf16[488,640]{1,0:T(8,128)(2,1)S(1)} collective-permute-done((bf16[488,640]{1,0:T(8,128)(2,1)S(1)}, bf16[488,640]{1,0:T(8,128)(2,1)S(1)}, u32[]{:S(2)}, u32[]{:S(2)}) %collective-permute-start.50) | collective-permute-done | bytes 624672 | tf_op jit(solution)/shard_map/ppermute | solution.py:86
  589.1 5.8 collective-permute-start.64
  597.9 7.2 %collective-permute-done.55 = bf16[488,640]{1,0:T(8,128)(2,1)S(1)} collective-permute-done((bf16[488,640]{1,0:T(8,128)(2,1)S(1)}, bf16[488,640]{1,0:T(8,128)(2,1)S(1)}, u32[]{:S(2)}, u32[]{:S(2)}) %collective-permute-start.55) | collective-permute-done | bytes 624672 | tf_op jit(solution)/shard_map/ppermute | solution.py:86
  605.3 4.6 collective-permute-done.57
  612.0 8.1 %collective-permute-start.65 = (bf16[488,640]{1,0:T(8,128)(2,1)S(1)}, bf16[488,640]{1,0:T(8,128)(2,1)S(1)}, u32[]{:S(2)}, u32[]{:S(2)}) collective-permute-start(bf16[488,640]{1,0:T(8,128)(2,1)S(1)} %get-tuple-element.151), channel_id=1, source_target_pairs={{0,2},{1,3},{2,4},{3,5},{4,6},{5,7},{8,10},{9,11},{10,12},{11,13},... | collective-permute-start | bytes 1873928 | tf_op jit(solution)/shard_map/ppermute | solution.py:98
  625.5 3.8 collective-permute-done.68
  (1082 shorter events, 282.1 us)
Async XLA Ops:
  3.0 5.3 collective-permute-start
  8.6 20.5 %collective-permute-start.1 = (bf16[488,640]{1,0:T(8,128)(2,1)S(1)}, bf16[488,640]{1,0:T(8,128)(2,1)}, u32[]{:S(2)}, u32[]{:S(2)}) collective-permute-start(bf16[488,640]{1,0:T(8,128)(2,1)S(1)} %pad_maximum_fusion.9.refs_1_), channel_id=1, source_target_pairs={{2,0},{3,1},{4,2},{5,3},{6,4},{7,5},{10,8},{11,9},{12,10},{13,11},... | collective-permute-start | bytes 1873928 | tf_op jit(solution)/shard_map/ppermute | solution.py:102
  9.9 17.3 %collective-permute-start.34 = (bf16[488,640]{1,0:T(8,128)(2,1)S(1)}, bf16[488,640]{1,0:T(8,128)(2,1)S(1)}, u32[]{:S(2)}, u32[]{:S(2)}) collective-permute-start(bf16[488,640]{1,0:T(8,128)(2,1)S(1)} %pad_maximum_fusion.9.refs_1_), channel_id=1, source_target_pairs={{0,8},{8,0},{16,24},{24,16},{1,9},{9,1},{17,25},{25,17},{2,10},{10... | collective-permute-start | bytes 1873928 | tf_op jit(solution)/shard_map/ppermute | solution.py:86
  12.8 23.2 %collective-permute-start.4 = (bf16[488,640]{1,0:T(8,128)(2,1)S(1)}, bf16[488,640]{1,0:T(8,128)(2,1)}, u32[]{:S(2)}, u32[]{:S(2)}) collective-permute-start(bf16[488,640]{1,0:T(8,128)(2,1)S(1)} %pad_maximum_fusion.9.refs_1_), channel_id=1, source_target_pairs={{0,2},{1,3},{2,4},{3,5},{4,6},{5,7},{8,10},{9,11},{10,12},{11,13},... | collective-permute-start | bytes 1873928 | tf_op jit(solution)/shard_map/ppermute | solution.py:98
  18.1 16.9 %collective-permute-start.35 = (bf16[488,640]{1,0:T(8,128)(2,1)S(1)}, bf16[488,640]{1,0:T(8,128)(2,1)S(1)}, u32[]{:S(2)}, u32[]{:S(2)}) collective-permute-start(bf16[488,640]{1,0:T(8,128)(2,1)S(1)} %pad_maximum_fusion.9.refs_1_), channel_id=1, source_target_pairs={{0,16},{8,24},{16,0},{24,8},{1,17},{9,25},{17,1},{25,9},{2,18},{10... | collective-permute-start | bytes 1873928 | tf_op jit(solution)/shard_map/ppermute | solution.py:90
  19.6 18.9 %collective-permute-start.38 = (bf16[488,640]{1,0:T(8,128)(2,1)S(1)}, bf16[488,640]{1,0:T(8,128)(2,1)S(1)}, u32[]{:S(2)}, u32[]{:S(2)}) collective-permute-start(bf16[488,640]{1,0:T(8,128)(2,1)S(1)} %pad_maximum_fusion.9.refs_1_), channel_id=1, source_target_pairs={{0,1},{1,0},{2,3},{3,2},{4,5},{5,4},{6,7},{7,6},{8,9},{9,8},{10,11... | collective-permute-start | bytes 1873928 | tf_op jit(solution)/shard_map/ppermute | solution.py:94
  27.2 14.1 %collective-permute-start.37 = (bf16[240,640]{1,0:T(8,128)(2,1)S(1)}, bf16[240,640]{1,0:T(8,128)(2,1)}, u32[]{:S(2)}, u32[]{:S(2)}) collective-permute-start(bf16[240,640]{1,0:T(8,128)(2,1)S(1)} %slice.786), channel_id=1, source_target_pairs={{0,16},{8,24},{16,0},{24,8},{1,17},{9,25},{17,1},{25,9},{2,18},{10... | collective-permute-start | bytes 921608 | tf_op jit(solution)/shard_map/ppermute | solution.py:90
  29.1 18.0 %collective-permute-start.2 = (bf16[488,640]{1,0:T(8,128)(2,1)}, bf16[488,640]{1,0:T(8,128)(2,1)}, u32[]{:S(2)}, u32[]{:S(2)}) collective-permute-start(bf16[488,640]{1,0:T(8,128)(2,1)} %collective-permute-done.1), channel_id=1, source_target_pairs={{2,0},{3,1},{4,2},{5,3},{10,8},{11,9},{12,10},{13,11},{18,16},{19,... | collective-permute-start | bytes 1873928 | tf_op jit(solution)/shard_map/ppermute | solution.py:102
  35.8 10.3 %collective-permute-start.36 = (bf16[248,640]{1,0:T(8,128)(2,1)}, bf16[248,640]{1,0:T(8,128)(2,1)S(1)}, u32[]{:S(2)}, u32[]{:S(2)}) collective-permute-start(bf16[248,640]{1,0:T(8,128)(2,1)} %slice.785), channel_id=1, source_target_pairs={{0,8},{8,0},{16,24},{24,16},{1,9},{9,1},{17,25},{25,17},{2,10},{10... | collective-permute-start | bytes 952328 | tf_op jit(solution)/shard_map/ppermute | solution.py:86
  35.9 11.9 %collective-permute-start.5 = (bf16[488,640]{1,0:T(8,128)(2,1)}, bf16[488,640]{1,0:T(8,128)(2,1)}, u32[]{:S(2)}, u32[]{:S(2)}) collective-permute-start(bf16[488,640]{1,0:T(8,128)(2,1)} %collective-permute-done.4), channel_id=1, source_target_pairs={{2,4},{3,5},{4,6},{5,7},{10,12},{11,13},{12,14},{13,15},{18,20},{1... | collective-permute-start | bytes 1873928 | tf_op jit(solution)/shard_map/ppermute | solution.py:98
  39.4 17.4 %collective-permute-start.25 = (bf16[488,640]{1,0:T(8,128)(2,1)S(1)}, bf16[488,640]{1,0:T(8,128)(2,1)S(1)}, u32[]{:S(2)}, u32[]{:S(2)}) collective-permute-start(bf16[488,640]{1,0:T(8,128)(2,1)S(1)} %broadcast_select_fusion.refs_1_), channel_id=1, source_target_pairs={{0,8},{8,0},{16,24},{24,16},{1,9},{9,1},{17,25},{25,17},{2,10},{10... | collective-permute-start | bytes 1873928 | tf_op jit(solution)/shard_map/ppermute | solution.py:86
  41.3 15.7 %collective-permute-start.26 = (bf16[488,640]{1,0:T(8,128)(2,1)S(1)}, bf16[488,640]{1,0:T(8,128)(2,1)S(1)}, u32[]{:S(2)}, u32[]{:S(2)}) collective-permute-start(bf16[488,640]{1,0:T(8,128)(2,1)S(1)} %broadcast_select_fusion.refs_1_), channel_id=1, source_target_pairs={{0,16},{8,24},{16,0},{24,8},{1,17},{9,25},{17,1},{25,9},{2,18},{10... | collective-permute-start | bytes 1873928 | tf_op jit(solution)/shard_map/ppermute | solution.py:90
  46.1 12.8 %collective-permute-start.29 = (bf16[488,640]{1,0:T(8,128)(2,1)S(1)}, bf16[488,640]{1,0:T(8,128)(2,1)}, u32[]{:S(2)}, u32[]{:S(2)}) collective-permute-start(bf16[488,640]{1,0:T(8,128)(2,1)S(1)} %broadcast_select_fusion.refs_1_), channel_id=1, source_target_pairs={{0,1},{1,0},{2,3},{3,2},{4,5},{5,4},{6,7},{7,6},{8,9},{9,8},{10,11... | collective-permute-start | bytes 1873928 | tf_op jit(solution)/shard_map/ppermute | solution.py:94
  47.1 13.4 %collective-permute-start.39 = (bf16[488,640]{1,0:T(8,128)(2,1)}, bf16[488,640]{1,0:T(8,128)(2,1)}, u32[]{:S(2)}, u32[]{:S(2)}) collective-permute-start(bf16[488,640]{1,0:T(8,128)(2,1)} %copy-done.6), channel_id=1, source_target_pairs={{0,1},{1,0},{2,3},{3,2},{4,5},{5,4},{6,7},{7,6},{8,9},{9,8},{10,11... | collective-permute-start | bytes 1873928 | tf_op jit(solution)/shard_map/ppermute | solution.py:94
  47.8 14.1 %collective-permute-start.40 = (bf16[488,640]{1,0:T(8,128)(2,1)S(1)}, bf16[488,640]{1,0:T(8,128)(2,1)}, u32[]{:S(2)}, u32[]{:S(2)}) collective-permute-start(bf16[488,640]{1,0:T(8,128)(2,1)S(1)} %collective-permute-done.35.refs_3_), channel_id=1, source_target_pairs={{0,1},{1,0},{2,3},{3,2},{4,5},{5,4},{6,7},{7,6},{8,9},{9,8},{10,11... | collective-permute-start | bytes 1873928 | tf_op jit(solution)/shard_map/ppermute | solution.py:94
  56.8 20.3 %collective-permute-start.16 = (bf16[488,640]{1,0:T(8,128)(2,1)S(1)}, bf16[488,640]{1,0:T(8,128)(2,1)S(1)}, u32[]{:S(2)}, u32[]{:S(2)}) collective-permute-start(bf16[488,640]{1,0:T(8,128)(2,1)S(1)} %select_select_fusion.1.refs_1_), channel_id=1, source_target_pairs={{0,8},{8,0},{16,24},{24,16},{1,9},{9,1},{17,25},{25,17},{2,10},{10... | collective-permute-start | bytes 1873928 | tf_op jit(solution)/shard_map/ppermute | solution.py:86
  57.1 19.5 %collective-permute-start.3 = (bf16[488,640]{1,0:T(8,128)(2,1)}, bf16[488,640]{1,0:T(8,128)(2,1)S(1)}, u32[]{:S(2)}, u32[]{:S(2)}) collective-permute-start(bf16[488,640]{1,0:T(8,128)(2,1)} %collective-permute-done.2), channel_id=1, source_target_pairs={{2,0},{3,1},{10,8},{11,9},{18,16},{19,17},{26,24},{27,25}} | collective-permute-start | bytes 1873928 | tf_op jit(solution)/shard_map/ppermute | solution.py:102
  59.0 7.9 %collective-permute-start.28 = (bf16[240,640]{1,0:T(8,128)(2,1)S(1)}, bf16[240,640]{1,0:T(8,128)(2,1)S(1)}, u32[]{:S(2)}, u32[]{:S(2)}) collective-permute-start(bf16[240,640]{1,0:T(8,128)(2,1)S(1)} %slice.784), channel_id=1, source_target_pairs={{0,16},{8,24},{16,0},{24,8},{1,17},{9,25},{17,1},{25,9},{2,18},{10... | collective-permute-start | bytes 921608 | tf_op jit(solution)/shard_map/ppermute | solution.py:90
  60.5 16.7 %collective-permute-start.6 = (bf16[488,640]{1,0:T(8,128)(2,1)}, bf16[488,640]{1,0:T(8,128)(2,1)S(1)}, u32[]{:S(2)}, u32[]{:S(2)}) collective-permute-start(bf16[488,640]{1,0:T(8,128)(2,1)} %collective-permute-done.5), channel_id=1, source_target_pairs={{4,6},{5,7},{12,14},{13,15},{20,22},{21,23},{28,30},{29,31}} | collective-permute-start | bytes 1873928 | tf_op jit(solution)/shard_map/ppermute | solution.py:98
  61.9 14.7 %collective-permute-start.27 = (bf16[248,640]{1,0:T(8,128)(2,1)S(1)}, bf16[248,640]{1,0:T(8,128)(2,1)S(1)}, u32[]{:S(2)}, u32[]{:S(2)}) collective-permute-start(bf16[248,640]{1,0:T(8,128)(2,1)S(1)} %slice.783), channel_id=1, source_target_pairs={{0,8},{8,0},{16,24},{24,16},{1,9},{9,1},{17,25},{25,17},{2,10},{10... | collective-permute-start | bytes 952328 | tf_op jit(solution)/shard_map/ppermute | solution.py:86
  66.8 12.4 %collective-permute-start.17 = (bf16[488,640]{1,0:T(8,128)(2,1)S(1)}, bf16[488,640]{1,0:T(8,128)(2,1)S(1)}, u32[]{:S(2)}, u32[]{:S(2)}) collective-permute-start(bf16[488,640]{1,0:T(8,128)(2,1)S(1)} %select_select_fusion.1.refs_1_), channel_id=1, source_target_pairs={{0,16},{8,24},{16,0},{24,8},{1,17},{9,25},{17,1},{25,9},{2,18},{10... | collective-permute-start | bytes 1873928 | tf_op jit(solution)/shard_map/ppermute | solution.py:90
  77.1 5.8 collective-permute-start.31
  77.2 10.2 %collective-permute-start.19 = (bf16[240,640]{1,0:T(8,128)(2,1)S(1)}, bf16[240,640]{1,0:T(8,128)(2,1)S(1)}, u32[]{:S(2)}, u32[]{:S(2)}) collective-permute-start(bf16[240,640]{1,0:T(8,128)(2,1)S(1)} %slice.782), channel_id=1, source_target_pairs={{0,16},{8,24},{16,0},{24,8},{1,17},{9,25},{17,1},{25,9},{2,18},{10... | collective-permute-start | bytes 921608 | tf_op jit(solution)/shard_map/ppermute | solution.py:90
  79.3 9.0 %collective-permute-start.33 = (bf16[240,640]{1,0:T(8,128)(2,1)S(1)}, bf16[240,640]{1,0:T(8,128)(2,1)S(1)}, u32[]{:S(2)}, u32[]{:S(2)}) collective-permute-start(bf16[240,640]{1,0:T(8,128)(2,1)S(1)} %collective-permute-done.28.refs_5_), channel_id=1, source_target_pairs={{0,1},{1,0},{2,3},{3,2},{4,5},{5,4},{6,7},{7,6},{8,9},{9,8},{10,11... | collective-permute-start | bytes 921608 | tf_op jit(solution)/shard_map/ppermute | solution.py:94
  79.3 24.8 %collective-permute-start.7 = (bf16[488,640]{1,0:T(8,128)(2,1)S(1)}, bf16[488,640]{1,0:T(8,128)(2,1)S(1)}, u32[]{:S(2)}, u32[]{:S(2)}) collective-permute-start(bf16[488,640]{1,0:T(8,128)(2,1)S(1)} %select_select_fusion.refs_1_), channel_id=1, source_target_pairs={{0,8},{8,0},{16,24},{24,16},{1,9},{9,1},{17,25},{25,17},{2,10},{10... | collective-permute-start | bytes 1873928 | tf_op jit(solution)/shard_map/ppermute | solution.py:86
  81.1 23.1 %collective-permute-start.8 = (bf16[488,640]{1,0:T(8,128)(2,1)S(1)}, bf16[488,640]{1,0:T(8,128)(2,1)S(1)}, u32[]{:S(2)}, u32[]{:S(2)}) collective-permute-start(bf16[488,640]{1,0:T(8,128)(2,1)S(1)} %select_select_fusion.refs_1_), channel_id=1, source_target_pairs={{0,16},{8,24},{16,0},{24,8},{1,17},{9,25},{17,1},{25,9},{2,18},{10... | collective-permute-start | bytes 1873928 | tf_op jit(solution)/shard_map/ppermute | solution.py:90
  82.9 19.7 %collective-permute-start.18 = (bf16[248,640]{1,0:T(8,128)(2,1)S(1)}, bf16[248,640]{1,0:T(8,128)(2,1)S(1)}, u32[]{:S(2)}, u32[]{:S(2)}) collective-permute-start(bf16[248,640]{1,0:T(8,128)(2,1)S(1)} %slice.781), channel_id=1, source_target_pairs={{0,8},{8,0},{16,24},{24,16},{1,9},{9,1},{17,25},{25,17},{2,10},{10... | collective-permute-start | bytes 952328 | tf_op jit(solution)/shard_map/ppermute | solution.py:86
  87.4 5.7 collective-permute-start.42
  88.3 15.3 %collective-permute-start.32 = (bf16[248,640]{1,0:T(8,128)(2,1)S(1)}, bf16[248,640]{1,0:T(8,128)(2,1)S(1)}, u32[]{:S(2)}, u32[]{:S(2)}) collective-permute-start(bf16[248,640]{1,0:T(8,128)(2,1)S(1)} %collective-permute-done.27.refs_4_), channel_id=1, source_target_pairs={{0,1},{1,0},{2,3},{3,2},{4,5},{5,4},{6,7},{7,6},{8,9},{9,8},{10,11... | collective-permute-start | bytes 952328 | tf_op jit(solution)/shard_map/ppermute | solution.py:94
  93.1 14.4 %collective-permute-start.21 = (bf16[488,640]{1,0:T(8,128)(2,1)S(1)}, bf16[488,640]{1,0:T(8,128)(2,1)S(1)}, u32[]{:S(2)}, u32[]{:S(2)}) collective-permute-start(bf16[488,640]{1,0:T(8,128)(2,1)S(1)} %collective-permute-done.16.refs_2_), channel_id=1, source_target_pairs={{0,1},{1,0},{2,3},{3,2},{4,5},{5,4},{6,7},{7,6},{8,9},{9,8},{10,11... | collective-permute-start | bytes 1873928 | tf_op jit(solution)/shard_map/ppermute | solution.py:94
  102.7 6.7 %collective-permute-start.22 = (bf16[488,640]{1,0:T(8,128)(2,1)S(1)}, bf16[488,640]{1,0:T(8,128)(2,1)S(1)}, u32[]{:S(2)}, u32[]{:S(2)}) collective-permute-start(bf16[488,640]{1,0:T(8,128)(2,1)S(1)} %collective-permute-done.17.refs_3_), channel_id=1, source_target_pairs={{0,1},{1,0},{2,3},{3,2},{4,5},{5,4},{6,7},{7,6},{8,9},{9,8},{10,11... | collective-permute-start | bytes 1873928 | tf_op jit(solution)/shard_map/ppermute | solution.py:94
  105.5 38.6 %collective-permute-start.11 = (bf16[488,640]{1,0:T(8,128)(2,1)S(1)}, bf16[488,640]{1,0:T(8,128)(2,1)S(1)}, u32[]{:S(2)}, u32[]{:S(2)}) collective-permute-start(bf16[488,640]{1,0:T(8,128)(2,1)S(1)} %select_select_fusion.refs_1_), channel_id=1, source_target_pairs={{0,1},{1,0},{2,3},{3,2},{4,5},{5,4},{6,7},{7,6},{8,9},{9,8},{10,11... | collective-permute-start | bytes 1873928 | tf_op jit(solution)/shard_map/ppermute | solution.py:94
  105.8 11.1 %collective-permute-start.9 = (bf16[248,640]{1,0:T(8,128)(2,1)S(1)}, bf16[248,640]{1,0:T(8,128)(2,1)S(1)}, u32[]{:S(2)}, u32[]{:S(2)}) collective-permute-start(bf16[248,640]{1,0:T(8,128)(2,1)S(1)} %slice.779), channel_id=1, source_target_pairs={{0,8},{8,0},{16,24},{24,16},{1,9},{9,1},{17,25},{25,17},{2,10},{10... | collective-permute-start | bytes 952328 | tf_op jit(solution)/shard_map/ppermute | solution.py:86
  107.6 9.3 %collective-permute-start.10 = (bf16[240,640]{1,0:T(8,128)(2,1)S(1)}, bf16[240,640]{1,0:T(8,128)(2,1)S(1)}, u32[]{:S(2)}, u32[]{:S(2)}) collective-permute-start(bf16[240,640]{1,0:T(8,128)(2,1)S(1)} %slice.780), channel_id=1, source_target_pairs={{0,16},{8,24},{16,0},{24,8},{1,17},{9,25},{17,1},{25,9},{2,18},{10... | collective-permute-start | bytes 921608 | tf_op jit(solution)/shard_map/ppermute | solution.py:90
  109.4 34.8 %collective-permute-start.12 = (bf16[488,640]{1,0:T(8,128)(2,1)S(1)}, bf16[488,640]{1,0:T(8,128)(2,1)S(1)}, u32[]{:S(2)}, u32[]{:S(2)}) collective-permute-start(bf16[488,640]{1,0:T(8,128)(2,1)S(1)} %collective-permute-done.7.refs_2_), channel_id=1, source_target_pairs={{0,1},{1,0},{2,3},{3,2},{4,5},{5,4},{6,7},{7,6},{8,9},{9,8},{10,11... | collective-permute-start | bytes 1873928 | tf_op jit(solution)/shard_map/ppermute | solution.py:94
  109.4 34.8 %collective-permute-start.13 = (bf16[488,640]{1,0:T(8,128)(2,1)S(1)}, bf16[488,640]{1,0:T(8,128)(2,1)S(1)}, u32[]{:S(2)}, u32[]{:S(2)}) collective-permute-start(bf16[488,640]{1,0:T(8,128)(2,1)S(1)} %collective-permute-done.8.refs_3_), channel_id=1, source_target_pairs={{0,1},{1,0},{2,3},{3,2},{4,5},{5,4},{6,7},{7,6},{8,9},{9,8},{10,11... | collective-permute-start | bytes 1873928 | tf_op jit(solution)/shard_map/ppermute | solution.py:94
  116.9 27.2 %collective-permute-start.15 = (bf16[240,640]{1,0:T(8,128)(2,1)S(1)}, bf16[240,640]{1,0:T(8,128)(2,1)S(1)}, u32[]{:S(2)}, u32[]{:S(2)}) collective-permute-start(bf16[240,640]{1,0:T(8,128)(2,1)S(1)} %collective-permute-done.10.refs_5_), channel_id=1, source_target_pairs={{0,1},{1,0},{2,3},{3,2},{4,5},{5,4},{6,7},{7,6},{8,9},{9,8},{10,11... | collective-permute-start | bytes 921608 | tf_op jit(solution)/shard_map/ppermute | solution.py:94
  116.9 27.3 %collective-permute-start.14 = (bf16[248,640]{1,0:T(8,128)(2,1)S(1)}, bf16[248,640]{1,0:T(8,128)(2,1)S(1)}, u32[]{:S(2)}, u32[]{:S(2)}) collective-permute-start(bf16[248,640]{1,0:T(8,128)(2,1)S(1)} %collective-permute-done.9.refs_4_), channel_id=1, source_target_pairs={{0,1},{1,0},{2,3},{3,2},{4,5},{5,4},{6,7},{7,6},{8,9},{9,8},{10,11... | collective-permute-start | bytes 952328 | tf_op jit(solution)/shard_map/ppermute | solution.py:94
  496.3 30.4 %collective-permute-start.58 = (bf16[4,488,640]{2,1,0:T(8,128)(2,1)}, bf16[4,488,640]{2,1,0:T(8,128)(2,1)}, u32[]{:S(2)}, u32[]{:S(2)}) collective-permute-start(bf16[4,488,640]{2,1,0:T(8,128)(2,1)} %get-tuple-element.67), channel_id=1, source_target_pairs={{0,1},{1,0},{2,3},{3,2},{4,5},{5,4},{6,7},{7,6},{8,9},{9,8},{10,11... | collective-permute-start | bytes 7495688 | tf_op jit(solution)/shard_map/ppermute | solution.py:94
  506.5 25.1 %collective-permute-start.48 = (bf16[4,488,640]{2,1,0:T(8,128)(2,1)S(1)}, bf16[4,488,640]{2,1,0:T(8,128)(2,1)}, u32[]{:S(2)}, u32[]{:S(2)}) collective-permute-start(bf16[4,488,640]{2,1,0:T(8,128)(2,1)S(1)} %get-tuple-element.63), channel_id=1, source_target_pairs={{0,1},{1,0},{2,3},{3,2},{4,5},{5,4},{6,7},{7,6},{8,9},{9,8},{10,11... | collective-permute-start | bytes 7495688 | tf_op jit(solution)/shard_map/ppermute | solution.py:94
  516.3 19.5 %collective-permute-start.53 = (bf16[4,488,640]{2,1,0:T(8,128)(2,1)S(1)}, bf16[4,488,640]{2,1,0:T(8,128)(2,1)}, u32[]{:S(2)}, u32[]{:S(2)}) collective-permute-start(bf16[4,488,640]{2,1,0:T(8,128)(2,1)S(1)} %get-tuple-element.65), channel_id=1, source_target_pairs={{0,1},{1,0},{2,3},{3,2},{4,5},{5,4},{6,7},{7,6},{8,9},{9,8},{10,11... | collective-permute-start | bytes 7495688 | tf_op jit(solution)/shard_map/ppermute | solution.py:94
  526.0 12.6 %collective-permute-start.43 = (bf16[4,488,640]{2,1,0:T(8,128)(2,1)S(1)}, bf16[4,488,640]{2,1,0:T(8,128)(2,1)S(1)}, u32[]{:S(2)}, u32[]{:S(2)}) collective-permute-start(bf16[4,488,640]{2,1,0:T(8,128)(2,1)S(1)} %get-tuple-element.61), channel_id=1, source_target_pairs={{0,1},{1,0},{2,3},{3,2},{4,5},{5,4},{6,7},{7,6},{8,9},{9,8},{10,11... | collective-permute-start | bytes 7495688 | tf_op jit(solution)/shard_map/ppermute | solution.py:94
  529.2 12.8 %collective-permute-start.61 = (bf16[248,640]{1,0:T(8,128)(2,1)S(1)}, bf16[248,640]{1,0:T(8,128)(2,1)S(1)}, u32[]{:S(2)}, u32[]{:S(2)}) collective-permute-start(bf16[248,640]{1,0:T(8,128)(2,1)S(1)} %get-tuple-element.166), channel_id=1, source_target_pairs={{0,8},{8,0},{16,24},{24,16},{1,9},{9,1},{17,25},{25,17},{2,10},{10... | collective-permute-start | bytes 952328 | tf_op jit(solution)/shard_map/ppermute | solution.py:86
  529.7 10.3 %collective-permute-start.59 = (bf16[240,640]{1,0:T(8,128)(2,1)S(1)}, bf16[240,640]{1,0:T(8,128)(2,1)S(1)}, u32[]{:S(2)}, u32[]{:S(2)}) collective-permute-start(bf16[240,640]{1,0:T(8,128)(2,1)S(1)} %get-tuple-element.167), channel_id=1, source_target_pairs={{0,16},{8,24},{16,0},{24,8},{1,17},{9,25},{17,1},{25,9},{2,18},{10... | collective-permute-start | bytes 921608 | tf_op jit(solution)/shard_map/ppermute | solution.py:90
  534.1 14.4 %collective-permute-start.51 = (bf16[248,640]{1,0:T(8,128)(2,1)S(1)}, bf16[248,640]{1,0:T(8,128)(2,1)S(1)}, u32[]{:S(2)}, u32[]{:S(2)}) collective-permute-start(bf16[248,640]{1,0:T(8,128)(2,1)S(1)} %get-tuple-element.162), channel_id=1, source_target_pairs={{0,8},{8,0},{16,24},{24,16},{1,9},{9,1},{17,25},{25,17},{2,10},{10... | collective-permute-start | bytes 952328 | tf_op jit(solution)/shard_map/ppermute | solution.py:86
  535.8 10.7 %collective-permute-start.49 = (bf16[240,640]{1,0:T(8,128)(2,1)S(1)}, bf16[240,640]{1,0:T(8,128)(2,1)S(1)}, u32[]{:S(2)}, u32[]{:S(2)}) collective-permute-start(bf16[240,640]{1,0:T(8,128)(2,1)S(1)} %get-tuple-element.163), channel_id=1, source_target_pairs={{0,16},{8,24},{16,0},{24,8},{1,17},{9,25},{17,1},{25,9},{2,18},{10... | collective-permute-start | bytes 921608 | tf_op jit(solution)/shard_map/ppermute | solution.py:90
  538.7 35.5 %collective-permute-start.56 = (bf16[248,640]{1,0:T(8,128)(2,1)S(1)}, bf16[248,640]{1,0:T(8,128)(2,1)S(1)}, u32[]{:S(2)}, u32[]{:S(2)}) collective-permute-start(bf16[248,640]{1,0:T(8,128)(2,1)S(1)} %get-tuple-element.158), channel_id=1, source_target_pairs={{0,8},{8,0},{16,24},{24,16},{1,9},{9,1},{17,25},{25,17},{2,10},{10... | collective-permute-start | bytes 952328 | tf_op jit(solution)/shard_map/ppermute | solution.py:86
  540.0 29.1 %collective-permute-start.54 = (bf16[240,640]{1,0:T(8,128)(2,1)S(1)}, bf16[240,640]{1,0:T(8,128)(2,1)S(1)}, u32[]{:S(2)}, u32[]{:S(2)}) collective-permute-start(bf16[240,640]{1,0:T(8,128)(2,1)S(1)} %get-tuple-element.159), channel_id=1, source_target_pairs={{0,16},{8,24},{16,0},{24,8},{1,17},{9,25},{17,1},{25,9},{2,18},{10... | collective-permute-start | bytes 921608 | tf_op jit(solution)/shard_map/ppermute | solution.py:90
  542.0 24.6 %collective-permute-start.60 = (bf16[488,640]{1,0:T(8,128)(2,1)S(1)}, bf16[488,640]{1,0:T(8,128)(2,1)S(1)}, u32[]{:S(2)}, u32[]{:S(2)}) collective-permute-start(bf16[488,640]{1,0:T(8,128)(2,1)S(1)} %pad_maximum_fusion.16), channel_id=1, source_target_pairs={{0,8},{8,0},{16,24},{24,16},{1,9},{9,1},{17,25},{25,17},{2,10},{10... | collective-permute-start | bytes 1873928 | tf_op jit(solution)/shard_map/ppermute | solution.py:86
  546.5 20.5 %collective-permute-start.62 = (bf16[488,640]{1,0:T(8,128)(2,1)S(1)}, bf16[488,640]{1,0:T(8,128)(2,1)S(1)}, u32[]{:S(2)}, u32[]{:S(2)}) collective-permute-start(bf16[488,640]{1,0:T(8,128)(2,1)S(1)} %pad_maximum_fusion.17), channel_id=1, source_target_pairs={{0,16},{8,24},{16,0},{24,8},{1,17},{9,25},{17,1},{25,9},{2,18},{10... | collective-permute-start | bytes 1873928 | tf_op jit(solution)/shard_map/ppermute | solution.py:90
  548.5 48.8 %collective-permute-start.46 = (bf16[248,640]{1,0:T(8,128)(2,1)S(1)}, bf16[248,640]{1,0:T(8,128)(2,1)S(1)}, u32[]{:S(2)}, u32[]{:S(2)}) collective-permute-start(bf16[248,640]{1,0:T(8,128)(2,1)S(1)} %get-tuple-element.154), channel_id=1, source_target_pairs={{0,8},{8,0},{16,24},{24,16},{1,9},{9,1},{17,25},{25,17},{2,10},{10... | collective-permute-start | bytes 952328 | tf_op jit(solution)/shard_map/ppermute | solution.py:86
  566.6 19.7 %collective-permute-start.50 = (bf16[488,640]{1,0:T(8,128)(2,1)S(1)}, bf16[488,640]{1,0:T(8,128)(2,1)S(1)}, u32[]{:S(2)}, u32[]{:S(2)}) collective-permute-start(bf16[488,640]{1,0:T(8,128)(2,1)S(1)} %pad_maximum_fusion.12), channel_id=1, source_target_pairs={{0,8},{8,0},{16,24},{24,16},{1,9},{9,1},{17,25},{25,17},{2,10},{10... | collective-permute-start | bytes 1873928 | tf_op jit(solution)/shard_map/ppermute | solution.py:86
  567.0 21.1 %collective-permute-start.52 = (bf16[488,640]{1,0:T(8,128)(2,1)S(1)}, bf16[488,640]{1,0:T(8,128)(2,1)S(1)}, u32[]{:S(2)}, u32[]{:S(2)}) collective-permute-start(bf16[488,640]{1,0:T(8,128)(2,1)S(1)} %pad_maximum_fusion.13), channel_id=1, source_target_pairs={{0,16},{8,24},{16,0},{24,8},{1,17},{9,25},{17,1},{25,9},{2,18},{10... | collective-permute-start | bytes 1873928 | tf_op jit(solution)/shard_map/ppermute | solution.py:90
  569.1 19.3 %collective-permute-start.63 = (bf16[488,640]{1,0:T(8,128)(2,1)S(1)}, bf16[488,640]{1,0:T(8,128)(2,1)S(1)}, u32[]{:S(2)}, u32[]{:S(2)}) collective-permute-start(bf16[488,640]{1,0:T(8,128)(2,1)S(1)} %fusion.60), channel_id=1, source_target_pairs={{0,2},{1,3},{8,10},{9,11},{16,18},{17,19},{24,26},{25,27}} | collective-permute-start | bytes 1873928 | tf_op jit(solution)/shard_map/ppermute | solution.py:98
  574.1 15.0 %collective-permute-start.66 = (bf16[488,640]{1,0:T(8,128)(2,1)S(1)}, bf16[488,640]{1,0:T(8,128)(2,1)S(1)}, u32[]{:S(2)}, u32[]{:S(2)}) collective-permute-start(bf16[488,640]{1,0:T(8,128)(2,1)S(1)} %fusion.60), channel_id=1, source_target_pairs={{6,4},{7,5},{14,12},{15,13},{22,20},{23,21},{30,28},{31,29}} | collective-permute-start | bytes 1873928 | tf_op jit(solution)/shard_map/ppermute | solution.py:102
  586.3 10.1 %collective-permute-start.44 = (bf16[240,640]{1,0:T(8,128)(2,1)S(1)}, bf16[240,640]{1,0:T(8,128)(2,1)S(1)}, u32[]{:S(2)}, u32[]{:S(2)}) collective-permute-start(bf16[240,640]{1,0:T(8,128)(2,1)S(1)} %get-tuple-element.155), channel_id=1, source_target_pairs={{0,16},{8,24},{16,0},{24,8},{1,17},{9,25},{17,1},{25,9},{2,18},{10... | collective-permute-start | bytes 921608 | tf_op jit(solution)/shard_map/ppermute | solution.py:90
  588.1 16.9 %collective-permute-start.55 = (bf16[488,640]{1,0:T(8,128)(2,1)S(1)}, bf16[488,640]{1,0:T(8,128)(2,1)S(1)}, u32[]{:S(2)}, u32[]{:S(2)}) collective-permute-start(bf16[488,640]{1,0:T(8,128)(2,1)S(1)} %pad_maximum_fusion.14), channel_id=1, source_target_pairs={{0,8},{8,0},{16,24},{24,16},{1,9},{9,1},{17,25},{25,17},{2,10},{10... | collective-permute-start | bytes 1873928 | tf_op jit(solution)/shard_map/ppermute | solution.py:86
  588.4 21.5 %collective-permute-start.57 = (bf16[488,640]{1,0:T(8,128)(2,1)S(1)}, bf16[488,640]{1,0:T(8,128)(2,1)S(1)}, u32[]{:S(2)}, u32[]{:S(2)}) collective-permute-start(bf16[488,640]{1,0:T(8,128)(2,1)S(1)} %pad_maximum_fusion.15), channel_id=1, source_target_pairs={{0,16},{8,24},{16,0},{24,8},{1,17},{9,25},{17,1},{25,9},{2,18},{10... | collective-permute-start | bytes 1873928 | tf_op jit(solution)/shard_map/ppermute | solution.py:90
  589.1 20.7 %collective-permute-start.64 = (bf16[488,640]{1,0:T(8,128)(2,1)S(1)}, bf16[488,640]{1,0:T(8,128)(2,1)S(1)}, u32[]{:S(2)}, u32[]{:S(2)}) collective-permute-start(bf16[488,640]{1,0:T(8,128)(2,1)S(1)} %get-tuple-element.129), channel_id=1, source_target_pairs={{0,2},{1,3},{2,4},{3,5},{8,10},{9,11},{10,12},{11,13},{16,18},{17,... | collective-permute-start | bytes 1873928 | tf_op jit(solution)/shard_map/ppermute | solution.py:98
  596.5 13.4 %collective-permute-start.67 = (bf16[488,640]{1,0:T(8,128)(2,1)S(1)}, bf16[488,640]{1,0:T(8,128)(2,1)S(1)}, u32[]{:S(2)}, u32[]{:S(2)}) collective-permute-start(bf16[488,640]{1,0:T(8,128)(2,1)S(1)} %add_convert_fusion.7), channel_id=1, source_target_pairs={{4,2},{5,3},{6,4},{7,5},{12,10},{13,11},{14,12},{15,13},{20,18},{2... | collective-permute-start | bytes 1873928 | tf_op jit(solution)/shard_map/ppermute | solution.py:102
  597.3 28.2 %collective-permute-start.45 = (bf16[488,640]{1,0:T(8,128)(2,1)S(1)}, bf16[488,640]{1,0:T(8,128)(2,1)S(1)}, u32[]{:S(2)}, u32[]{:S(2)}) collective-permute-start(bf16[488,640]{1,0:T(8,128)(2,1)S(1)} %pad_maximum_fusion.10), channel_id=1, source_target_pairs={{0,8},{8,0},{16,24},{24,16},{1,9},{9,1},{17,25},{25,17},{2,10},{10... | collective-permute-start | bytes 1873928 | tf_op jit(solution)/shard_map/ppermute | solution.py:86
  605.0 20.5 %collective-permute-start.47 = (bf16[488,640]{1,0:T(8,128)(2,1)S(1)}, bf16[488,640]{1,0:T(8,128)(2,1)S(1)}, u32[]{:S(2)}, u32[]{:S(2)}) collective-permute-start(bf16[488,640]{1,0:T(8,128)(2,1)S(1)} %pad_maximum_fusion.11), channel_id=1, source_target_pairs={{0,16},{8,24},{16,0},{24,8},{1,17},{9,25},{17,1},{25,9},{2,18},{10... | collective-permute-start | bytes 1873928 | tf_op jit(solution)/shard_map/ppermute | solution.py:90
  610.5 18.8 %collective-permute-start.68 = (bf16[488,640]{1,0:T(8,128)(2,1)S(1)}, bf16[488,640]{1,0:T(8,128)(2,1)S(1)}, u32[]{:S(2)}, u32[]{:S(2)}) collective-permute-start(bf16[488,640]{1,0:T(8,128)(2,1)S(1)} %get-tuple-element.152), channel_id=1, source_target_pairs={{2,0},{3,1},{4,2},{5,3},{6,4},{7,5},{10,8},{11,9},{12,10},{13,11},... | collective-permute-start | bytes 1873928 | tf_op jit(solution)/shard_map/ppermute | solution.py:102
  612.0 18.4 %collective-permute-start.65 = (bf16[488,640]{1,0:T(8,128)(2,1)S(1)}, bf16[488,640]{1,0:T(8,128)(2,1)S(1)}, u32[]{:S(2)}, u32[]{:S(2)}) collective-permute-start(bf16[488,640]{1,0:T(8,128)(2,1)S(1)} %get-tuple-element.151), channel_id=1, source_target_pairs={{0,2},{1,3},{2,4},{3,5},{4,6},{5,7},{8,10},{9,11},{10,12},{11,13},... | collective-permute-start | bytes 1873928 | tf_op jit(solution)/shard_map/ppermute | solution.py:98
  (327 other events, 1796.1 us)
